TPU v7x, 32 devices: a whole 2x2x4 slice. The times are simulated.
32 devices in a mesh: dp: 4 (over y, x), ctx: 8 (over z, core).
Axes of the slice: x: 2, y: 2, z: 4, core: 2. Of those that a mesh axis runs over, the one named last changes fastest.
Arguments:
- block_input: bfloat16 [4, 1024, 1024], P('dp', 'ctx'), may hold values from -6 to 6
- segment_ids: int32 [4, 1024], P('dp', 'ctx'), may hold values from 0 to 3, never falling along the last dimension, each value on 1 to 512 neighbouring positions
- out_cotangent: bfloat16 [4, 1024, 1024], P('dp', 'ctx'), may hold values from -6 to 6
- attention_in: bfloat16 [1024, 768], P(('dp', 'ctx')), may hold values from -0.1875 to 0.1875
- mixer_in: bfloat16 [1024, 3328], P(('dp', 'ctx')), may hold values from -0.1875 to 0.1875
- step_in: bfloat16 [1024, 24], P(('dp', 'ctx')), may hold values from -0.1875 to 0.1875
- attention_out: bfloat16 [512, 1024], P(('dp', 'ctx')), may hold values from -2 to 2
- mixer_out: bfloat16 [1536, 1024], P(('dp', 'ctx')), may hold values from -0.3125 to 0.3125
- gate_up: bfloat16 [1024, 4096], P(('dp', 'ctx')), may hold values from -0.1875 to 0.1875
- down_weight: bfloat16 [2048, 1024], P(('dp', 'ctx')), may hold values from -0.125 to 0.125
- gain_mixing: float32 [1024], replicated, may hold values from 0.5 to 1.5
- gain_feed: float32 [1024], replicated, may hold values from 0.5 to 1.5
- decay_log: float32 [24], replicated, may hold values from 0 to 2.77
- step_bias: float32 [24], replicated, may hold values from -6.9 to -2.25
- skip_gain: float32 [24], replicated, may hold values from 0.5 to 2
- conv_weight: float32 [4, 1792], replicated, may hold values from -2 to 2
- conv_bias: float32 [1792], replicated, may hold values from -0.5 to 0.5
Outputs:
- output: bfloat16 [4, 1024, 1024], P('dp', 'ctx')
- input_grad: float32 [4, 1024, 1024], P('dp', 'ctx')
- grad_attention_in: float32 [1024, 768], P(('dp', 'ctx'))
- grad_mixer_in: float32 [1024, 3328], P(('dp', 'ctx'))
- grad_step_in: float32 [1024, 24], P(('dp', 'ctx'))
- grad_attention_out: float32 [512, 1024], P(('dp', 'ctx'))
- grad_mixer_out: float32 [1536, 1024], P(('dp', 'ctx'))
- grad_gate_up: float32 [1024, 4096], P(('dp', 'ctx'))
- grad_down_weight: float32 [2048, 1024], P(('dp', 'ctx'))
- grad_gain_mixing: float32 [1024], replicated
- grad_gain_feed: float32 [1024], replicated
- grad_decay_log: float32 [24], replicated
- grad_step_bias: float32 [24], replicated
- grad_skip_gain: float32 [24], replicated
- grad_conv_weight: float32 [4, 1792], replicated
- grad_conv_bias: float32 [1792], replicated
Inputs may be any that keep to these rules, and one draw needn't show every extreme that they name: `segment_ids`: segment ids never fall along a sequence; each document holds 1 to 512 tokens and one holds exactly 512.
All inputs are finite; a program needn't handle non-finite values.
Results may differ from a plain program's by a relative error of at most 0.013.
Values may be sent and summed in bfloat16 or wider, within the bound.
A program may use at most 192 MiB of HBM per device.

v0:
```python
import jax
import jax.numpy as jnp
from jax import lax
from jax.sharding import PartitionSpec as P

FF = 2048
HEADS_Q = 8
HEADS_KV = 2
HEAD = 64
SSM_HEADS = 24
SSM_HEAD = 64
STATE = 128
SSM_INNER = 1536


highest = lax.Precision.HIGHEST


def from_behind(block, axis, distance):
    devices = range(lax.axis_size(axis))
    route = [(i - distance, i) for i in devices if i - distance in devices]
    return lax.ppermute(block, axis, route)


def carried_in(value, axis, join, neutral, backward):
    count, mine = (lax.axis_size(axis), lax.axis_index(axis))
    pieces = jax.tree.map(lambda part: lax.all_gather(part, axis), value)
    if backward:
        pieces = jax.tree.map(lambda part: part[::-1], pieces)
        mine = count - 1 - mine
    so_far = jax.tree.map(
        lambda part, zero: jnp.full_like(part, 0) + jnp.asarray(zero, part.dtype), value, neutral
    )

    def hop(position, so_far):
        longer = join(so_far, jax.tree.map(lambda part: part[position], pieces))
        return jax.tree.map(lambda new, old: jnp.where(position < mine, new, old), longer, so_far)

    return lax.fori_loop(0, count - 1, hop, so_far)


def rms_scale(values, gain):
    return values * lax.rsqrt(jnp.mean(values * values, axis=-1, keepdims=True) + 1e-05) * gain


def silu_slope(values):
    sigma = jax.nn.sigmoid(values)
    return sigma * (1.0 + values * (1.0 - sigma))


def ssd_local(
    inner, write_map, read_map, step_raw, decay_log, step_bias, skip_gain, starts, segments
):
    step = jax.nn.softplus(step_raw + step_bias)
    rates = step * -jnp.exp(decay_log)
    running = jnp.cumsum(rates, axis=0)
    places = jnp.arange(segments.shape[0])
    same = (segments[:, None] == segments[None, :]) & (places[None, :] <= places[:, None])
    spans = jnp.where(same[None], running.T[:, :, None] - running.T[:, None, :], -1e30)
    intersection = jnp.dot(read_map, write_map.T, precision=highest)
    mixing = jnp.exp(spans) * intersection[None] * step.T[:, None, :]
    result = (
        jnp.einsum("hts,shp->thp", mixing, inner, precision=highest)
        + skip_gain[None, :, None] * inner
    )
    before = jnp.cumsum(starts.astype(jnp.int32)) == 0
    carried = jnp.where(before[:, None], jnp.exp(running), 0.0)
    tails = jnp.where(
        (segments == segments[-1])[:, None], jnp.exp(running[-1][None, :] - running), 0.0
    )
    state = jnp.einsum("sh,shp,sn->hpn", tails * step, inner, write_map, precision=highest)
    return (result, state, carried[-1], carried)


def add_state(result, carried, read_map, state_in):
    return result + carried[:, :, None] * jnp.einsum(
        "hpn,tn->thp", state_in, read_map, precision=highest
    )


def ssd_block(
    inner,
    write_map,
    read_map,
    step_raw,
    decay_log,
    step_bias,
    skip_gain,
    starts,
    segments,
    state_in,
):
    result, state, decay_total, carried = ssd_local(
        inner, write_map, read_map, step_raw, decay_log, step_bias, skip_gain, starts, segments
    )
    return (
        add_state(result, carried, read_map, state_in),
        decay_total[:, None, None] * state_in + state,
    )


def chain(earlier, later):
    return (earlier[0] * later[0], later[0][:, :, None, None] * earlier[1] + later[1])


def group_queries(flat, seq_count, tok_count):
    groups = HEADS_Q // HEADS_KV
    shaped = flat.reshape(seq_count, tok_count, HEADS_KV, groups, HEAD)
    return shaped.transpose(0, 2, 3, 1, 4).reshape(seq_count, HEADS_KV, groups * tok_count, HEAD)


def ungroup(grouped, seq_count, tok_count):
    groups = HEADS_Q // HEADS_KV
    shaped = grouped.reshape(seq_count, HEADS_KV, groups, tok_count, HEAD)
    return shaped.transpose(0, 3, 1, 2, 4).reshape(seq_count * tok_count, HEADS_Q * HEAD)


def local(
    block_input,
    segment_ids,
    out_cotangent,
    attention_in,
    mixer_in,
    step_in,
    attention_out,
    mixer_out,
    gate_up,
    down_weight,
    gain_mixing,
    gain_feed,
    decay_log,
    step_bias,
    skip_gain,
    conv_weight,
    conv_bias,
):
    seq_count, tok_count, width = block_input.shape
    row_count = seq_count * tok_count
    length = tok_count * lax.axis_size("ctx")
    block = min(512, length)
    blocks = length // block
    groups = HEADS_Q // HEADS_KV
    query_width = HEADS_Q * HEAD
    key_width = HEADS_KV * HEAD
    score_scale = HEAD ** (-0.5)
    query_rows = groups * tok_count
    first = lax.axis_index("ctx") * tok_count
    gathered = (
        lax.all_gather(attention_in, ("dp", "ctx"), axis=0, tiled=True),
        lax.all_gather(mixer_in, ("dp", "ctx"), axis=0, tiled=True),
        lax.all_gather(step_in, ("dp", "ctx"), axis=0, tiled=True),
        lax.all_gather(attention_out, ("dp", "ctx"), axis=0, tiled=True),
        lax.all_gather(mixer_out, ("dp", "ctx"), axis=0, tiled=True),
        lax.all_gather(gate_up, ("dp", "ctx"), axis=0, tiled=True),
        lax.all_gather(down_weight, ("dp", "ctx"), axis=0, tiled=True),
    )
    (
        full_attention_in,
        full_mixer_in,
        full_step_in,
        full_attention_out,
        full_mixer_out,
        full_gate_up,
        full_down,
    ) = gathered
    source = block_input.reshape(row_count, width).astype(jnp.float32)
    normed = rms_scale(source, gain_mixing).astype(jnp.bfloat16)
    projected = jnp.dot(normed, full_attention_in, preferred_element_type=jnp.float32).astype(
        jnp.bfloat16
    )
    mixed_in = jnp.dot(normed, full_mixer_in, preferred_element_type=jnp.float32)
    step_raw = jnp.dot(normed, full_step_in, preferred_element_type=jnp.float32).reshape(
        seq_count, tok_count, SSM_HEADS
    )
    queries = group_queries(projected[:, :query_width], seq_count, tok_count)
    local_keys = (
        projected[:, query_width:].reshape(seq_count, tok_count, 2 * key_width).transpose(1, 0, 2)
    )
    local_segments = segment_ids.T
    keys_all, segments_all = (
        lax.all_gather(local_keys, "ctx", axis=0, tiled=True),
        lax.all_gather(local_segments, "ctx", axis=0, tiled=True),
    )
    query_pos = first + jnp.arange(query_rows) % tok_count
    query_segments = jnp.tile(segment_ids, (1, groups))
    segment_blocks = segments_all.reshape(blocks, block, seq_count)
    block_ids = jnp.arange(blocks)

    def scores_of(key_block, seg_block, block_id):
        keys = key_block[:, :, :key_width].reshape(block, seq_count, HEADS_KV, HEAD)
        scores = (
            jnp.einsum("sgrd,ksgd->sgrk", queries, keys, preferred_element_type=jnp.float32)
            * score_scale
        )
        key_pos = block_id * block + jnp.arange(block)
        allowed = (key_pos[None, None, None, :] <= query_pos[None, None, :, None]) & (
            seg_block.T[:, None, None, :] == query_segments[:, None, :, None]
        )
        return (scores, allowed)

    key_blocks = keys_all.reshape(blocks, block, seq_count, 2 * key_width)

    def gather_stats(carry, item):
        top, total = carry
        scores, allowed = scores_of(item[0], item[1], item[2])
        masked = jnp.where(allowed, scores, -1e30)
        new_top = jnp.maximum(top, jnp.max(masked, axis=-1))
        total = total * jnp.exp(top - new_top) + jnp.sum(
            jnp.where(allowed, jnp.exp(masked - new_top[..., None]), 0.0), axis=-1
        )
        return ((new_top, total), None)

    start_top = jnp.full((seq_count, HEADS_KV, query_rows), -1e30, jnp.float32)
    (top, total), _ = lax.scan(
        gather_stats,
        (start_top, jnp.zeros_like(start_top)),
        (key_blocks, segment_blocks, block_ids),
    )
    log_total = top + jnp.log(total)

    def weigh_values(accum, item):
        scores, allowed = scores_of(item[0], item[1], item[2])
        values = item[0][:, :, key_width:].reshape(block, seq_count, HEADS_KV, HEAD)
        probs = jnp.where(allowed, jnp.exp(scores - log_total[..., None]), 0.0).astype(jnp.bfloat16)
        return (
            accum
            + jnp.einsum("sgrk,ksgd->sgrd", probs, values, preferred_element_type=jnp.float32),
            None,
        )

    attended, _ = lax.scan(
        weigh_values, jnp.zeros(queries.shape, jnp.float32), (key_blocks, segment_blocks, block_ids)
    )
    attended = attended.astype(jnp.bfloat16)
    attended_flat = ungroup(attended, seq_count, tok_count)
    gate_part = mixed_in[:, :SSM_INNER]
    conv_width = mixed_in.shape[1] - SSM_INNER
    conv_in = mixed_in[:, SSM_INNER:].reshape(seq_count, tok_count, conv_width)
    positions = first + jnp.arange(tok_count)
    before_rows = from_behind(conv_in[:, tok_count - 3 :, :], "ctx", 1)
    extended = jnp.concatenate([before_rows, conv_in], axis=1)
    pre = conv_bias + conv_weight[3] * conv_in
    keep_masks = []
    for offset in (1, 2, 3):
        earlier_ids = segments_all[jnp.maximum(positions - offset, 0)].T
        keep_mask = (positions >= offset)[None, :] & (earlier_ids == segment_ids)
        keep_masks.append(keep_mask)
        pre = (
            pre
            + jnp.where(keep_mask[..., None], extended[:, 3 - offset : 3 - offset + tok_count], 0.0)
            * conv_weight[3 - offset]
        )
    converted = jax.nn.silu(pre)
    inner = converted[..., :SSM_INNER].reshape(seq_count, tok_count, SSM_HEADS, SSM_HEAD)
    write_map = converted[..., SSM_INNER : SSM_INNER + STATE]
    read_map = converted[..., SSM_INNER + STATE :]
    starts = (positions == 0)[None, :] | jnp.logical_not(keep_masks[0])
    local_map = jax.vmap(ssd_local, in_axes=(0, 0, 0, 0, None, None, None, 0, 0))
    partial_out, partial_state, decay_total, carried = local_map(
        inner, write_map, read_map, step_raw, decay_log, step_bias, skip_gain, starts, segment_ids
    )
    unit = (jnp.ones_like(decay_total), jnp.zeros_like(partial_state))
    scanned_in = carried_in((decay_total, partial_state), "ctx", chain, unit, False)
    state_in = scanned_in[1]
    scanned = jax.vmap(add_state)(partial_out, carried, read_map, state_in)
    flat_scan = scanned.reshape(row_count, SSM_INNER)
    gated = (flat_scan * jax.nn.silu(gate_part)).astype(jnp.bfloat16)
    residual = (
        source
        + jnp.dot(attended_flat, full_attention_out, preferred_element_type=jnp.float32)
        + jnp.dot(gated, full_mixer_out, preferred_element_type=jnp.float32)
    )
    normed_two = rms_scale(residual, gain_feed).astype(jnp.bfloat16)
    gate_values = jnp.dot(normed_two, full_gate_up, preferred_element_type=jnp.float32)
    gate_in = gate_values[:, :FF]
    up_in = gate_values[:, FF:]
    active = (jax.nn.silu(gate_in) * up_in).astype(jnp.bfloat16)
    output = (residual + jnp.dot(active, full_down, preferred_element_type=jnp.float32)).astype(
        jnp.bfloat16
    )
    back_weights = (
        lax.all_gather(attention_in, ("dp", "ctx"), axis=0, tiled=True),
        lax.all_gather(mixer_in, ("dp", "ctx"), axis=0, tiled=True),
        lax.all_gather(step_in, ("dp", "ctx"), axis=0, tiled=True),
        lax.all_gather(attention_out, ("dp", "ctx"), axis=0, tiled=True),
        lax.all_gather(mixer_out, ("dp", "ctx"), axis=0, tiled=True),
        lax.all_gather(gate_up, ("dp", "ctx"), axis=0, tiled=True),
        lax.all_gather(down_weight, ("dp", "ctx"), axis=0, tiled=True),
    )
    keys_back = lax.all_gather(local_keys, "ctx", axis=0, tiled=True)
    (
        back_attention_in,
        back_mixer_in,
        back_step_in,
        back_attention_out,
        back_mixer_out,
        back_gate_up,
        back_down,
    ) = back_weights
    cotangent = out_cotangent.reshape(row_count, width)
    grad_down_weight = jnp.dot(active.T, cotangent, preferred_element_type=jnp.float32)
    active_grad = jnp.dot(cotangent, back_down.T, preferred_element_type=jnp.float32)
    gate_grad = jnp.concatenate(
        [active_grad * up_in * silu_slope(gate_in), active_grad * jax.nn.silu(gate_in)], axis=1
    ).astype(jnp.bfloat16)
    grad_gate_up = jnp.dot(normed_two.T, gate_grad, preferred_element_type=jnp.float32)
    normed_two_grad = jnp.dot(gate_grad, back_gate_up.T, preferred_element_type=jnp.float32)
    _, pull_two = jax.vjp(rms_scale, residual, gain_feed)
    residual_part, grad_gain_feed = pull_two(normed_two_grad)
    residual_grad = cotangent.astype(jnp.float32) + residual_part
    residual_half = residual_grad.astype(jnp.bfloat16)
    grad_attention_out = jnp.dot(attended_flat.T, residual_half, preferred_element_type=jnp.float32)
    grad_mixer_out = jnp.dot(gated.T, residual_half, preferred_element_type=jnp.float32)
    attended_grad = jnp.dot(
        residual_half, back_attention_out.T, preferred_element_type=jnp.float32
    ).astype(jnp.bfloat16)
    gated_grad = jnp.dot(residual_half, back_mixer_out.T, preferred_element_type=jnp.float32)
    gate_part_grad = gated_grad * flat_scan * silu_slope(gate_part)
    scan_grad = (gated_grad * jax.nn.silu(gate_part)).reshape(
        seq_count, tok_count, SSM_HEADS, SSM_HEAD
    )
    direct = jnp.einsum("sth,sthp,stn->shpn", carried, scan_grad, read_map, precision=highest)
    scanned_back = carried_in((decay_total, direct), "ctx", chain, unit, True)
    state_grad = scanned_back[1]

    def block_map(inner_v, write_v, read_v, step_v, decay_v, bias_v, skip_v, state_v):
        mapped = jax.vmap(ssd_block, in_axes=(0, 0, 0, 0, None, None, None, 0, 0, 0))
        return mapped(
            inner_v, write_v, read_v, step_v, decay_v, bias_v, skip_v, starts, segment_ids, state_v
        )

    _, pull_scan = jax.vjp(
        block_map, inner, write_map, read_map, step_raw, decay_log, step_bias, skip_gain, state_in
    )
    pulled = pull_scan((scan_grad, state_grad))
    converted_grad = jnp.concatenate(
        [pulled[0].reshape(seq_count, tok_count, SSM_INNER), pulled[1], pulled[2]], axis=2
    )
    pre_grad = converted_grad * silu_slope(pre)
    after_rows = from_behind(pre_grad[:, :3, :], "ctx", -1)
    ahead = jnp.concatenate([pre_grad, after_rows], axis=1)
    conv_in_grad = conv_weight[3] * pre_grad
    tap_grads = [None, None, None, jnp.sum(pre_grad * conv_in, axis=(0, 1))]
    for offset in (1, 2, 3):
        later_ids = segments_all[jnp.minimum(positions + offset, length - 1)].T
        later_mask = later_ids == segment_ids
        conv_in_grad = (
            conv_in_grad
            + jnp.where(later_mask[..., None], ahead[:, offset : offset + tok_count], 0.0)
            * conv_weight[3 - offset]
        )
        earlier_rows = jnp.where(
            keep_masks[offset - 1][..., None], extended[:, 3 - offset : 3 - offset + tok_count], 0.0
        )
        tap_grads[3 - offset] = jnp.sum(pre_grad * earlier_rows, axis=(0, 1))
    grad_conv_weight = jnp.stack(tap_grads, axis=0)
    grad_conv_bias = jnp.sum(pre_grad, axis=(0, 1))
    mixer_grad = jnp.concatenate(
        [gate_part_grad, conv_in_grad.reshape(row_count, conv_width)], axis=1
    ).astype(jnp.bfloat16)
    step_grad_half = pulled[3].reshape(row_count, SSM_HEADS).astype(jnp.bfloat16)
    out_grad = group_queries(attended_grad, seq_count, tok_count)
    deltas = jnp.sum(out_grad.astype(jnp.float32) * attended.astype(jnp.float32), axis=-1)
    back_blocks = keys_back.reshape(blocks, block, seq_count, 2 * key_width)

    def attention_grads(query_grad, item):
        scores, allowed = scores_of(item[0], item[1], item[2])
        keys = item[0][:, :, :key_width].reshape(block, seq_count, HEADS_KV, HEAD)
        values = item[0][:, :, key_width:].reshape(block, seq_count, HEADS_KV, HEAD)
        probs = jnp.where(allowed, jnp.exp(scores - log_total[..., None]), 0.0)
        value_grad = jnp.einsum(
            "sgrk,sgrd->ksgd",
            probs.astype(jnp.bfloat16),
            out_grad,
            preferred_element_type=jnp.float32,
        )
        prob_grad = jnp.einsum(
            "sgrd,ksgd->sgrk", out_grad, values, preferred_element_type=jnp.float32
        )
        score_grad = (probs * (prob_grad - deltas[..., None])).astype(jnp.bfloat16)
        query_grad = (
            query_grad
            + jnp.einsum("sgrk,ksgd->sgrd", score_grad, keys, preferred_element_type=jnp.float32)
            * score_scale
        )
        key_grad = (
            jnp.einsum("sgrk,sgrd->ksgd", score_grad, queries, preferred_element_type=jnp.float32)
            * score_scale
        )
        both = jnp.concatenate(
            [
                key_grad.reshape(block, seq_count, key_width),
                value_grad.reshape(block, seq_count, key_width),
            ],
            axis=2,
        )
        return (query_grad, both)

    query_grad, key_terms = lax.scan(
        attention_grads,
        jnp.zeros(queries.shape, jnp.float32),
        (back_blocks, segment_blocks, block_ids),
    )
    key_sums = lax.psum_scatter(
        key_terms.reshape(length, seq_count, 2 * key_width).astype(jnp.bfloat16),
        "ctx",
        scatter_dimension=0,
        tiled=True,
    ).astype(jnp.float32)
    kv_grad = key_sums.transpose(1, 0, 2).reshape(row_count, 2 * key_width)
    projected_grad = jnp.concatenate(
        [ungroup(query_grad, seq_count, tok_count), kv_grad], axis=1
    ).astype(jnp.bfloat16)
    grad_attention_in = jnp.dot(normed.T, projected_grad, preferred_element_type=jnp.float32)
    grad_mixer_in = jnp.dot(normed.T, mixer_grad, preferred_element_type=jnp.float32)
    grad_step_in = jnp.dot(normed.T, step_grad_half, preferred_element_type=jnp.float32)
    normed_grad = (
        jnp.dot(projected_grad, back_attention_in.T, preferred_element_type=jnp.float32)
        + jnp.dot(mixer_grad, back_mixer_in.T, preferred_element_type=jnp.float32)
        + jnp.dot(step_grad_half, back_step_in.T, preferred_element_type=jnp.float32)
    )
    _, pull_one = jax.vjp(rms_scale, source, gain_mixing)
    source_part, grad_gain_mixing = pull_one(normed_grad)
    input_grad = residual_grad + source_part
    weight_sums = (
        lax.psum_scatter(grad_attention_in, ("dp", "ctx"), scatter_dimension=0, tiled=True),
        lax.psum_scatter(grad_mixer_in, ("dp", "ctx"), scatter_dimension=0, tiled=True),
        lax.psum_scatter(grad_step_in, ("dp", "ctx"), scatter_dimension=0, tiled=True),
        lax.psum_scatter(grad_attention_out, ("dp", "ctx"), scatter_dimension=0, tiled=True),
        lax.psum_scatter(grad_mixer_out, ("dp", "ctx"), scatter_dimension=0, tiled=True),
        lax.psum_scatter(grad_gate_up, ("dp", "ctx"), scatter_dimension=0, tiled=True),
        lax.psum_scatter(grad_down_weight, ("dp", "ctx"), scatter_dimension=0, tiled=True),
    )
    small_sums = lax.psum(
        (
            grad_gain_mixing,
            grad_gain_feed,
            pulled[4],
            pulled[5],
            pulled[6],
            grad_conv_weight,
            grad_conv_bias,
        ),
        ("dp", "ctx"),
    )
    return (
        output.reshape(seq_count, tok_count, width),
        input_grad.reshape(seq_count, tok_count, width),
        weight_sums[0],
        weight_sums[1],
        weight_sums[2],
        weight_sums[3],
        weight_sums[4],
        weight_sums[5],
        weight_sums[6],
        small_sums[0],
        small_sums[1],
        small_sums[2],
        small_sums[3],
        small_sums[4],
        small_sums[5],
        small_sums[6],
    )


def solution(mesh):
    in_specs = (
        P("dp", "ctx", None),
        P("dp", "ctx"),
        P("dp", "ctx", None),
        P(("dp", "ctx"), None),
        P(("dp", "ctx"), None),
        P(("dp", "ctx"), None),
        P(("dp", "ctx"), None),
        P(("dp", "ctx"), None),
        P(("dp", "ctx"), None),
        P(("dp", "ctx"), None),
        P(),
        P(),
        P(),
        P(),
        P(),
        P(),
        P(),
    )
    out_specs = (
        P("dp", "ctx", None),
        P("dp", "ctx", None),
        P(("dp", "ctx"), None),
        P(("dp", "ctx"), None),
        P(("dp", "ctx"), None),
        P(("dp", "ctx"), None),
        P(("dp", "ctx"), None),
        P(("dp", "ctx"), None),
        P(("dp", "ctx"), None),
        P(),
        P(),
        P(),
        P(),
        P(),
        P(),
        P(),
    )
    return jax.shard_map(local, mesh=mesh, in_specs=in_specs, out_specs=out_specs, check_vma=False)
```

profile of v0, /device:TPU:0, one launch (start us, length us, event | category | flops | bytes accessed | tf_op | source)
XLA Modules:
  0.0 1594.4 jit_solution(12975452984190645541)
XLA Ops:
  9.4 13.6 all-gather
  26.5 39.1 %all-gather.4 = bf16[32,32,24]{1,2,0:T(8,128)(2,1)S(1)} all-gather(bf16[1,32,24]{1,2,0:T(8,128)(2,1)} %bitcast.614), channel_id=1, replica_groups=mesh['dp'=4,'ctx'=8] {'dp','ctx'}, dimensions={0}, use_global_device_ids=true | all-gather | bytes 50688 | tf_op jit(solution)/shard_map/all_gather | solution.py:151
  76.0 9.0 all-gather.18.cloned.1.call-done
  99.4 12.4 all_gather.57
  113.2 28.4 %all-gather.14.cloned.1.call-done = bf16[1024,768]{1,0:T(8,128)(2,1)} async-done(((bf16[32,768]{1,0:T(8,128)(2,1)}), bf16[1024,768]{1,0:T(8,128)(2,1)}) %all-gather.14.cloned.1.call-update) | async-done | bytes 1572880 | tf_op jit(solution)/shard_map/all_gather | solution.py:149
  143.4 14.8 all-gather.1
  160.0 9.4 while.65
  170.1 10.3 while.66
  181.4 15.9 all-gather.16.cloned.1.call-done
  201.4 61.1 %all-gather.26.cloned.1.call-done = f32[192,64,128]{2,1,0:T(8,128)} async-done(((f32[24,64,128]{2,1,0:T(8,128)}), f32[192,64,128]{2,1,0:T(8,128)}) %all-gather.26.cloned.1.call-update) | async-done | bytes 6291472 | tf_op jit(solution)/shard_map/all_gather | solution.py:27
  262.5 9.9 while.67
  275.1 5.1 fusion.68
  282.6 40.7 %all-gather.20.cloned.1.call-done = bf16[1536,1024]{1,0:T(8,128)(2,1)} async-done(((bf16[48,1024]{1,0:T(8,128)(2,1)}), bf16[1536,1024]{1,0:T(8,128)(2,1)}) %all-gather.20.cloned.1.call-update) | async-done | bytes 3145744 | tf_op jit(solution)/shard_map/all_gather | solution.py:153
  326.6 75.3 %all-gather.22.cloned.1.call-done = bf16[1024,4096]{1,0:T(8,128)(2,1)} async-done(((bf16[32,4096]{1,0:T(8,128)(2,1)}), bf16[1024,4096]{1,0:T(8,128)(2,1)}) %all-gather.22.cloned.1.call-update) | async-done | bytes 8388624 | tf_op jit(solution)/shard_map/all_gather | solution.py:154
  402.0 6.1 fusion.204
  408.0 57.3 %all-gather.24.cloned.1.call-done = bf16[2048,1024]{1,0:T(8,128)(2,1)} async-done(((bf16[64,1024]{1,0:T(8,128)(2,1)}), bf16[2048,1024]{1,0:T(8,128)(2,1)}) %all-gather.24.cloned.1.call-update) | async-done | bytes 4194320 | tf_op jit(solution)/shard_map/all_gather | solution.py:155
  465.3 5.4 multiply_convert_fusion.1
  490.8 21.5 %while.68 = (s32[]{:T(128)}, f32[1,2,512,64]{2,3,1,0:T(8,128)}, bf16[2,512,1,256]{3,1,0,2:T(8,128)(2,1)}, s32[2]{0:T(128)}, s32[2,512,1]{1,2,0:T(1,128)S(1)}, /*...) while((s32[]{:T(128)}, f32[1,2,512,64]{2,3,1,0:T(8,128)}, ...), condition=%wide.region_15.16_spmd.clone, body=%wide.region_14.15_spmd.clone.sunk | while | flops 340856832 | bytes 19032864 | solution.py:399
  512.4 33.0 %all-gather.28.cloned.1.call-done = f32[192,64,128]{2,1,0:T(8,128)} async-done(((f32[24,64,128]{2,1,0:T(8,128)}), f32[192,64,128]{2,1,0:T(8,128)}) %all-gather.28.cloned.1.call-update) | async-done | bytes 6291472 | tf_op jit(solution)/shard_map/all_gather | solution.py:27
  545.4 6.7 rev.7
  552.1 13.8 while.69
  592.3 9.4 fusion.122
  631.1 6.9 fusion.130
  643.2 5.3 fusion.131
  649.8 39.2 %all-reduce.2 = (f32[1024]{0:T(1024)}, f32[1024]{0:T(1024)}, f32[24]{0:T(128)}, f32[24]{0:T(128)}, f32[24]{0:T(128)}, /*index=5*/f32[4,1792]{1,0:T(4,128)}, f32[1792]{0:T(1024)}) all-reduce(f32[1024]{0:T(1024)S(1)} %get-tuple-element.726, f32[1024]{0:T(1024)S(1)} %copy-done.89, ...), channel_id=1, replica_groups=mesh['dp'=4,'ctx'=8] {'dp','ctx'}, use_global_device_ids=true, to_apply=%region_36.37 | all-reduce | flops 11080 | bytes 88640 | tf_op jit(solution)/shard_map/psum | solution.py:434
  690.1 23.8 %reduce-scatter.27.cloned.1.call-done = f32[32,24]{1,0:T(8,128)} async-done(((f32[1024,24]{1,0:T(8,128)}), f32[32,24]{1,0:T(8,128)}) %reduce-scatter.27.cloned.1.call-update) | async-done | bytes 3088
  715.3 136.6 %reduce-scatter.17.cloned.1.call-done = f32[16,1024]{1,0:T(8,128)} async-done(((f32[512,1024]{1,0:T(8,128)}), f32[16,1024]{1,0:T(8,128)}) %reduce-scatter.17.cloned.1.call-update) | async-done | bytes 65552 | tf_op jit(solution)/shard_map/reduce_scatter | solution.py:429
  851.9 104.3 %reduce-scatter.13.cloned.1.call-done = f32[32,768]{1,0:T(8,128)} async-done(((f32[1024,768]{1,0:T(8,128)}), f32[32,768]{1,0:T(8,128)}) %reduce-scatter.13.cloned.1.call-update) | async-done | bytes 98320 | tf_op jit(solution)/shard_map/reduce_scatter | solution.py:426
  956.2 120.2 %reduce-scatter.19.cloned.1.call-done = f32[48,1024]{1,0:T(8,128)} async-done(((f32[1536,1024]{1,0:T(8,128)}), f32[48,1024]{1,0:T(8,128)}) %reduce-scatter.19.cloned.1.call-update) | async-done | bytes 196624 | tf_op jit(solution)/shard_map/reduce_scatter | solution.py:430
  1076.4 155.1 %reduce-scatter.23.cloned.1.call-done = f32[64,1024]{1,0:T(8,128)} async-done(((f32[2048,1024]{1,0:T(8,128)}), f32[64,1024]{1,0:T(8,128)}) %reduce-scatter.23.cloned.1.call-update) | async-done | bytes 262160 | tf_op jit(solution)/shard_map/reduce_scatter | solution.py:432
  1231.5 187.2 %reduce-scatter.21.cloned.1.call-done = f32[32,4096]{1,0:T(8,128)} async-done(((f32[1024,4096]{1,0:T(8,128)}), f32[32,4096]{1,0:T(8,128)}) %reduce-scatter.21.cloned.1.call-update) | async-done | bytes 524304 | tf_op jit(solution)/shard_map/reduce_scatter | solution.py:431
  1418.7 168.8 %reduce-scatter.15.cloned.1.call-done = f32[32,3328]{1,0:T(8,128)} async-done(((f32[1024,3328]{1,0:T(8,128)}), f32[32,3328]{1,0:T(8,128)}) %reduce-scatter.15.cloned.1.call-update) | async-done | bytes 426000 | tf_op jit(solution)/shard_map/reduce_scatter | solution.py:427
  (516 shorter events, 192.8 us)
Async XLA Ops:
  7.2 77.7 %all-gather.18.cloned.1.call-start = ((), (), s32[]{:S(2)}) async-start(), calls=%async_computation.10 | async-start | bytes 7028736 | tf_op jit(solution)/shard_map/all_gather | solution.py:150
  7.9 133.6 %all-gather.14.cloned.1.call-start = ((), (), s32[]{:S(2)}) async-start(), calls=%async_computation.8 | async-start | bytes 1622016 | tf_op jit(solution)/shard_map/all_gather | solution.py:149
  8.7 188.6 %all-gather.16.cloned.1.call-start = ((), (), s32[]{:S(2)}) async-start(), calls=%async_computation.9 | async-start | bytes 1081344 | tf_op jit(solution)/shard_map/all_gather | solution.py:152
  9.4 253.1 %all-gather.26.cloned.1.call-start = ((), (), s32[]{:S(2)}) async-start(), calls=%async_computation.20 | async-start | bytes 7077888 | tf_op jit(solution)/shard_map/all_gather | solution.py:27
  25.8 115.7 %copy-start.83 = (f32[128]{0:T(128)}, f32[128]{0:T(128)S(1)}, u32[]{:S(2)}) copy-start(f32[128]{0:T(128)S(1)} %fusion.193) | copy-start | bytes 1540
  26.4 40.7 %copy-start.112 = (f32[24]{0:T(128)}, f32[24]{0:T(128)S(1)}, u32[]{:S(2)}) copy-start(f32[24]{0:T(128)S(1)} %exponential_negate_fusion) | copy-start | bytes 292
  67.1 21.8 %copy-start.57 = (f32[128,24]{0,1:T(8,128)}, f32[128,24]{0,1:T(8,128)S(1)}, u32[]{:S(2)}) copy-start(f32[128,24]{0,1:T(8,128)S(1)} %convolution_add_fusion.6) | copy-start | bytes 36868
  67.5 30.5 %copy-start.53 = (f32[1,128,24]{1,2,0:T(8,128)}, f32[1,128,24]{1,2,0:T(8,128)S(1)}, u32[]{:S(2)}) copy-start(f32[1,128,24]{1,2,0:T(8,128)S(1)} %copy.216) | copy-start | bytes 36868
  75.2 22.8 %copy-start.101 = (pred[128]{0:T(512)(128)(4,1)}, pred[128]{0:T(512)(128)(4,1)S(1)}, u32[]{:S(2)}) copy-start(pred[128]{0:T(512)(128)(4,1)S(1)} %compare_reduce_fusion) | copy-start | bytes 388
  89.1 3.0 collective-permute-start
  94.3 49.0 %copy-start.6 = (f32[1,128,1536]{1,2,0:T(8,128)}, f32[1,128,1536]{1,2,0:T(8,128)S(1)}, u32[]{:S(2)}) copy-start(f32[1,128,1536]{1,2,0:T(8,128)S(1)} %copy.209) | copy-start | bytes 2359300
  96.0 227.3 %all-gather.20.cloned.1.call-start = ((), (), s32[]{:S(2)}) async-start(), calls=%async_computation.11 | async-start | bytes 3244032 | tf_op jit(solution)/shard_map/all_gather | solution.py:153
  96.6 305.4 %all-gather.22.cloned.1.call-start = ((), (), s32[]{:S(2)}) async-start(), calls=%async_computation.12 | async-start | bytes 8650752 | tf_op jit(solution)/shard_map/all_gather | solution.py:154
  97.2 368.1 %all-gather.24.cloned.1.call-start = ((), (), s32[]{:S(2)}) async-start(), calls=%async_computation.13 | async-start | bytes 4325376 | tf_op jit(solution)/shard_map/all_gather | solution.py:155
  97.9 447.5 %all-gather.28.cloned.1.call-start = ((), (), s32[]{:S(2)}) async-start(), calls=%async_computation.21 | async-start | bytes 7077888 | tf_op jit(solution)/shard_map/all_gather | solution.py:27
  181.4 81.1 %copy-start.42 = (bf16[1,128,2,4,64]{1,4,3,2,0:T(8,128)(2,1)}, bf16[1,128,2,4,64]{1,4,3,2,0:T(8,128)(2,1)S(1)}, u32[]{:S(2)}) copy-start(bf16[1,128,2,4,64]{1,4,3,2,0:T(8,128)(2,1)S(1)} %copy.208) | copy-start | bytes 393220
  282.6 119.4 %copy-start.45 = (f32[1024]{0:T(1024)S(1)}, f32[1024]{0:T(1024)}, u32[]{:S(2)}) copy-start(f32[1024]{0:T(1024)} %param.38) | copy-start | bytes 12292
  326.1 75.9 %copy-start.118 = (f32[128]{0:T(128)}, f32[128]{0:T(128)S(1)}, u32[]{:S(2)}) copy-start(f32[128]{0:T(128)S(1)} %get-tuple-element.857) | copy-start | bytes 1540
  326.1 148.2 %copy-start.4 = (f32[128,1024]{1,0:T(8,128)}, f32[128,1024]{1,0:T(8,128)S(1)}, u32[]{:S(2)}) copy-start(f32[128,1024]{1,0:T(8,128)S(1)} %get-tuple-element.858) | copy-start | bytes 1572868
  402.0 63.3 %copy-start.35 = (bf16[1,128,1024]{2,1,0:T(8,128)(2,1)S(1)}, bf16[1,128,1024]{2,1,0:T(8,128)(2,1)}, u32[]{:S(2)}) copy-start(bf16[1,128,1024]{2,1,0:T(8,128)(2,1)} %param.29) | copy-start | bytes 786436
  481.8 95.9 %reduce-scatter.25.cloned.1.call-start = ((), (), s32[]{:S(2)}) async-start(), calls=%async_computation.22 | async-start | bytes 589824
  512.4 201.5 %reduce-scatter.27.cloned.1.call-start = ((), (), s32[]{:S(2)}) async-start(), calls=%async_computation.23 | async-start | bytes 540672
  572.6 279.3 %reduce-scatter.17.cloned.1.call-start = ((), (), s32[]{:S(2)}) async-start(), calls=%async_computation.16 | async-start | bytes 2162688 | tf_op jit(solution)/shard_map/reduce_scatter | solution.py:429
  574.4 381.7 %reduce-scatter.13.cloned.1.call-start = ((), (), s32[]{:S(2)}) async-start(), calls=%async_computation.14 | async-start | bytes 3244032 | tf_op jit(solution)/shard_map/reduce_scatter | solution.py:426
  581.0 495.3 %reduce-scatter.19.cloned.1.call-start = ((), (), s32[]{:S(2)}) async-start(), calls=%async_computation.17 | async-start | bytes 6488064 | tf_op jit(solution)/shard_map/reduce_scatter | solution.py:430
  585.6 645.8 %reduce-scatter.23.cloned.1.call-start = ((), (), s32[]{:S(2)}) async-start(), calls=%async_computation.19 | async-start | bytes 8650752 | tf_op jit(solution)/shard_map/reduce_scatter | solution.py:432
  591.3 827.4 %reduce-scatter.21.cloned.1.call-start = ((), (), s32[]{:S(2)}) async-start(), calls=%async_computation.18 | async-start | bytes 17301504 | tf_op jit(solution)/shard_map/reduce_scatter | solution.py:431
  601.8 985.6 %reduce-scatter.15.cloned.1.call-start = ((), (), s32[]{:S(2)}) async-start(), calls=%async_computation.15 | async-start | bytes 14057472 | tf_op jit(solution)/shard_map/reduce_scatter | solution.py:427
  627.3 3.1 collective-permute-start.1
  648.6 40.3 %copy-start.117 = (f32[128]{0:T(128)S(1)}, f32[128]{0:T(128)}, u32[]{:S(2)}) copy-start(f32[128]{0:T(128)} %copy-done.116) | copy-start | bytes 1540
  648.6 40.3 %copy-start.25 = (f32[128,1024]{1,0:T(8,128)S(1)}, f32[128,1024]{1,0:T(8,128)}, u32[]{:S(2)}) copy-start(f32[128,1024]{1,0:T(8,128)} %copy-done.24) | copy-start | bytes 1572868
  648.6 40.3 %copy-start.107 = (f32[128]{0:T(128)S(1)}, f32[128]{0:T(128)}, u32[]{:S(2)}) copy-start(f32[128]{0:T(128)} %copy-done.106) | copy-start | bytes 1540
  (110 other events, 554.5 us)
Sparse Core Ops, SparseCore 0:
  10.8 74.0 all-gather.17
  87.9 53.5 all-gather.13
  144.5 52.7 all-gather.15
  198.8 63.6 all-gather.25
  265.4 57.8 all-gather.19
  326.1 75.7 all-gather.21
  405.0 60.2 all-gather.23
  481.9 63.4 all-gather.27
  547.7 29.9 reduce-scatter.24
  579.8 134.0 reduce-scatter.26
  716.7 135.1 reduce-scatter.16
  857.7 98.3 reduce-scatter.12
  962.4 113.9 reduce-scatter.18
  1079.1 152.3 reduce-scatter.22
  1234.2 184.4 reduce-scatter.20
  1421.4 165.9 reduce-scatter.14
where the time goes:
time: 1610 us; the launch traced here: 1590 us
  waiting for transfers between devices  1230 us (76%)
  matrix products  125 us (8%)
  blocking collectives  119 us (7%)
  local copies, waits for them, and re-layouts  54.8 us (3%)
  other arithmetic  44.3 us (3%)
    reduce_scatter x1, waiting for transfers between devices, local(): lax.psum_scatter(grad_gate_up, ('dp', 'ctx'), scatter_dimension=0, tiled=...  187 us
    reduce_scatter x1, waiting for transfers between devices, local(): lax.psum_scatter(grad_mixer_in, ('dp', 'ctx'), scatter_dimension=0, tiled...  169 us
    reduce_scatter x1, waiting for transfers between devices, local(): lax.psum_scatter(grad_down_weight, ('dp', 'ctx'), scatter_dimension=0, ti...  155 us
    reduce_scatter x1, waiting for transfers between devices, local(): lax.psum_scatter(grad_attention_out, ('dp', 'ctx'), scatter_dimension=0,...  137 us
    reduce_scatter x1, waiting for transfers between devices, local(): lax.psum_scatter(grad_mixer_out, ('dp', 'ctx'), scatter_dimension=0, tile...  120 us
    reduce_scatter x1, waiting for transfers between devices, local(): lax.psum_scatter(grad_attention_in, ('dp', 'ctx'), scatter_dimension=0, t...  104 us
    all_gather x2, waiting for transfers between devices, carried_in(): pieces = jax.tree.map(lambda part: lax.all_gather(part, axis), value)  94.1 us
    all_gather x1, waiting for transfers between devices, local(): lax.all_gather(gate_up, ('dp', 'ctx'), axis=0, tiled=True)  75.3 us
  transfers between devices with their start and end apart: 18, of which 18 were waited for; matrix products, arithmetic and copies ran while one was open for 13% of the time, Pallas kernels for 0%

commit v1 on v0

--- a/solution.py
+++ b/solution.py
@@ -1,3 +1,5 @@
+import math
+
 import jax
 import jax.numpy as jnp
 from jax import lax
@@ -37,6 +39,67 @@
         return jax.tree.map(lambda new, old: jnp.where(position < mine, new, old), longer, so_far)
 
     return lax.fori_loop(0, count - 1, hop, so_far)
+
+
+def carried_by_heads(decays, state, backward):
+    count, mine = (lax.axis_size("ctx"), lax.axis_index("ctx"))
+    seq_count, heads = decays.shape[1:]
+    share = heads // count
+    own = lax.dynamic_slice_in_dim(decays, mine * share, share, axis=2)
+    pieces = lax.all_to_all(state, "ctx", split_axis=1, concat_axis=0, tiled=True)
+    pieces = pieces.reshape((count, seq_count, share) + state.shape[2:])
+    order = list(range(count))[::-1] if backward else list(range(count))
+    so_far = jnp.zeros_like(pieces[0])
+    reached = [None] * count
+    for position in order:
+        reached[position] = so_far
+        so_far = own[position][:, :, None, None] * so_far + pieces[position]
+    return lax.all_to_all(
+        jnp.concatenate(reached, axis=0), "ctx", split_axis=0, concat_axis=1, tiled=True
+    )
+
+
+def fold_shape(owned, rows, width):
+    step = math.gcd(owned, rows)
+    return (step, owned // step, rows // step, width // (rows // step))
+
+
+def fold_rows(array, owned, rows):
+    step, across, down, part = fold_shape(owned, rows, array.shape[1])
+    blocks = array.reshape(-1, owned, array.shape[1])
+    columns = [
+        jnp.concatenate(
+            [blocks[:, i * step : (i + 1) * step, j * part : (j + 1) * part] for j in range(down)],
+            axis=1,
+        )
+        for i in range(across)
+    ]
+    return jnp.concatenate(columns, axis=2).reshape(-1, across * part)
+
+
+def unfold_rows(array, owned, rows, width):
+    step, across, down, part = fold_shape(owned, rows, width)
+    blocks = array.reshape(-1, rows, across * part)
+    lines = [
+        jnp.concatenate(
+            [blocks[:, j * step : (j + 1) * step, i * part : (i + 1) * part] for j in range(down)],
+            axis=2,
+        )
+        for i in range(across)
+    ]
+    return jnp.concatenate(lines, axis=1).reshape(-1, width)
+
+
+def pad_columns(array):
+    return jnp.pad(array, ((0, 0), (0, -array.shape[1] % 128)))
+
+
+def cut_columns(array, widths):
+    pieces, at = ([], 0)
+    for width in widths:
+        pieces.append(array[:, at : at + width])
+        at += width
+    return pieces
 
 
 def rms_scale(values, gain):
@@ -101,6 +164,13 @@
 
 def chain(earlier, later):
     return (earlier[0] * later[0], later[0][:, :, None, None] * earlier[1] + later[1])
+
+
+def over_blocks(step, start, items):
+    if items[2].shape[0] > 1:
+        return lax.scan(step, start, items)
+    carry, result = step(start, (items[0][0], items[1][0], 0))
+    return (carry, None if result is None else result[None])
 
 
 def group_queries(flat, seq_count, tok_count):
@@ -137,7 +207,7 @@
     seq_count, tok_count, width = block_input.shape
     row_count = seq_count * tok_count
     length = tok_count * lax.axis_size("ctx")
-    block = min(512, length)
+    block = length if length <= 1024 else 512
     blocks = length // block
     groups = HEADS_Q // HEADS_KV
     query_width = HEADS_Q * HEAD
@@ -145,24 +215,23 @@
     score_scale = HEAD ** (-0.5)
     query_rows = groups * tok_count
     first = lax.axis_index("ctx") * tok_count
-    gathered = (
-        lax.all_gather(attention_in, ("dp", "ctx"), axis=0, tiled=True),
-        lax.all_gather(mixer_in, ("dp", "ctx"), axis=0, tiled=True),
-        lax.all_gather(step_in, ("dp", "ctx"), axis=0, tiled=True),
-        lax.all_gather(attention_out, ("dp", "ctx"), axis=0, tiled=True),
-        lax.all_gather(mixer_out, ("dp", "ctx"), axis=0, tiled=True),
-        lax.all_gather(gate_up, ("dp", "ctx"), axis=0, tiled=True),
-        lax.all_gather(down_weight, ("dp", "ctx"), axis=0, tiled=True),
-    )
-    (
-        full_attention_in,
-        full_mixer_in,
-        full_step_in,
-        full_attention_out,
-        full_mixer_out,
-        full_gate_up,
-        full_down,
-    ) = gathered
+    own_rows = attention_in.shape[0]
+    axes = ("dp", "ctx")
+    entry = jnp.concatenate([attention_in, mixer_in, pad_columns(step_in)], axis=1)
+    full_attention_in, full_mixer_in, full_step_in = cut_columns(
+        lax.all_gather(entry, axes, axis=0, tiled=True),
+        (attention_in.shape[1], mixer_in.shape[1], step_in.shape[1]),
+    )
+    tall = (attention_out, mixer_out, down_weight)
+    folded = [fold_rows(weight, weight.shape[0], own_rows) for weight in tall]
+    rest = lax.all_gather(
+        jnp.concatenate(folded + [gate_up], axis=1), axes, axis=0, tiled=True
+    )
+    rest = cut_columns(rest, [weight.shape[1] for weight in folded] + [gate_up.shape[1]])
+    full_attention_out, full_mixer_out, full_down = (
+        unfold_rows(part, weight.shape[0], own_rows, width) for part, weight in zip(rest, tall)
+    )
+    full_gate_up = rest[3]
     source = block_input.reshape(row_count, width).astype(jnp.float32)
     normed = rms_scale(source, gain_mixing).astype(jnp.bfloat16)
     projected = jnp.dot(normed, full_attention_in, preferred_element_type=jnp.float32).astype(
@@ -211,7 +280,7 @@
         return ((new_top, total), None)
 
     start_top = jnp.full((seq_count, HEADS_KV, query_rows), -1e30, jnp.float32)
-    (top, total), _ = lax.scan(
+    (top, total), _ = over_blocks(
         gather_stats,
         (start_top, jnp.zeros_like(start_top)),
         (key_blocks, segment_blocks, block_ids),
@@ -228,7 +297,7 @@
             None,
         )
 
-    attended, _ = lax.scan(
+    attended, _ = over_blocks(
         weigh_values, jnp.zeros(queries.shape, jnp.float32), (key_blocks, segment_blocks, block_ids)
     )
     attended = attended.astype(jnp.bfloat16)
@@ -259,9 +328,13 @@
     partial_out, partial_state, decay_total, carried = local_map(
         inner, write_map, read_map, step_raw, decay_log, step_bias, skip_gain, starts, segment_ids
     )
-    unit = (jnp.ones_like(decay_total), jnp.zeros_like(partial_state))
-    scanned_in = carried_in((decay_total, partial_state), "ctx", chain, unit, False)
-    state_in = scanned_in[1]
+    by_heads = SSM_HEADS % lax.axis_size("ctx") == 0
+    if by_heads:
+        decays = lax.all_gather(decay_total, "ctx")
+        state_in = carried_by_heads(decays, partial_state, False)
+    else:
+        unit = (jnp.ones_like(decay_total), jnp.zeros_like(partial_state))
+        state_in = carried_in((decay_total, partial_state), "ctx", chain, unit, False)[1]
     scanned = jax.vmap(add_state)(partial_out, carried, read_map, state_in)
     flat_scan = scanned.reshape(row_count, SSM_INNER)
     gated = (flat_scan * jax.nn.silu(gate_part)).astype(jnp.bfloat16)
@@ -278,33 +351,26 @@
     output = (residual + jnp.dot(active, full_down, preferred_element_type=jnp.float32)).astype(
         jnp.bfloat16
     )
-    back_weights = (
-        lax.all_gather(attention_in, ("dp", "ctx"), axis=0, tiled=True),
-        lax.all_gather(mixer_in, ("dp", "ctx"), axis=0, tiled=True),
-        lax.all_gather(step_in, ("dp", "ctx"), axis=0, tiled=True),
-        lax.all_gather(attention_out, ("dp", "ctx"), axis=0, tiled=True),
-        lax.all_gather(mixer_out, ("dp", "ctx"), axis=0, tiled=True),
-        lax.all_gather(gate_up, ("dp", "ctx"), axis=0, tiled=True),
-        lax.all_gather(down_weight, ("dp", "ctx"), axis=0, tiled=True),
-    )
-    keys_back = lax.all_gather(local_keys, "ctx", axis=0, tiled=True)
-    (
-        back_attention_in,
-        back_mixer_in,
-        back_step_in,
-        back_attention_out,
-        back_mixer_out,
-        back_gate_up,
-        back_down,
-    ) = back_weights
     cotangent = out_cotangent.reshape(row_count, width)
-    grad_down_weight = jnp.dot(active.T, cotangent, preferred_element_type=jnp.float32)
-    active_grad = jnp.dot(cotangent, back_down.T, preferred_element_type=jnp.float32)
+    grad_down_weight = jnp.dot(active.T, cotangent, preferred_element_type=jnp.float32).astype(
+        jnp.bfloat16
+    )
+    active_grad = jnp.dot(cotangent, full_down.T, preferred_element_type=jnp.float32)
     gate_grad = jnp.concatenate(
         [active_grad * up_in * silu_slope(gate_in), active_grad * jax.nn.silu(gate_in)], axis=1
     ).astype(jnp.bfloat16)
-    grad_gate_up = jnp.dot(normed_two.T, gate_grad, preferred_element_type=jnp.float32)
-    normed_two_grad = jnp.dot(gate_grad, back_gate_up.T, preferred_element_type=jnp.float32)
+    grad_gate_up = jnp.dot(normed_two.T, gate_grad, preferred_element_type=jnp.float32).astype(
+        jnp.bfloat16
+    )
+    feed_sums = lax.psum_scatter(
+        jnp.concatenate(
+            [grad_gate_up, fold_rows(grad_down_weight, down_weight.shape[0], own_rows)], axis=1
+        ),
+        axes,
+        scatter_dimension=0,
+        tiled=True,
+    )
+    normed_two_grad = jnp.dot(gate_grad, full_gate_up.T, preferred_element_type=jnp.float32)
     _, pull_two = jax.vjp(rms_scale, residual, gain_feed)
     residual_part, grad_gain_feed = pull_two(normed_two_grad)
     residual_grad = cotangent.astype(jnp.float32) + residual_part
@@ -312,16 +378,18 @@
     grad_attention_out = jnp.dot(attended_flat.T, residual_half, preferred_element_type=jnp.float32)
     grad_mixer_out = jnp.dot(gated.T, residual_half, preferred_element_type=jnp.float32)
     attended_grad = jnp.dot(
-        residual_half, back_attention_out.T, preferred_element_type=jnp.float32
+        residual_half, full_attention_out.T, preferred_element_type=jnp.float32
     ).astype(jnp.bfloat16)
-    gated_grad = jnp.dot(residual_half, back_mixer_out.T, preferred_element_type=jnp.float32)
+    gated_grad = jnp.dot(residual_half, full_mixer_out.T, preferred_element_type=jnp.float32)
     gate_part_grad = gated_grad * flat_scan * silu_slope(gate_part)
     scan_grad = (gated_grad * jax.nn.silu(gate_part)).reshape(
         seq_count, tok_count, SSM_HEADS, SSM_HEAD
     )
     direct = jnp.einsum("sth,sthp,stn->shpn", carried, scan_grad, read_map, precision=highest)
-    scanned_back = carried_in((decay_total, direct), "ctx", chain, unit, True)
-    state_grad = scanned_back[1]
+    if by_heads:
+        state_grad = carried_by_heads(decays, direct, True)
+    else:
+        state_grad = carried_in((decay_total, direct), "ctx", chain, unit, True)[1]
 
     def block_map(inner_v, write_v, read_v, step_v, decay_v, bias_v, skip_v, state_v):
         mapped = jax.vmap(ssd_block, in_axes=(0, 0, 0, 0, None, None, None, 0, 0, 0))
@@ -361,7 +429,6 @@
     step_grad_half = pulled[3].reshape(row_count, SSM_HEADS).astype(jnp.bfloat16)
     out_grad = group_queries(attended_grad, seq_count, tok_count)
     deltas = jnp.sum(out_grad.astype(jnp.float32) * attended.astype(jnp.float32), axis=-1)
-    back_blocks = keys_back.reshape(blocks, block, seq_count, 2 * key_width)
 
     def attention_grads(query_grad, item):
         scores, allowed = scores_of(item[0], item[1], item[2])
@@ -396,10 +463,10 @@
         )
         return (query_grad, both)
 
-    query_grad, key_terms = lax.scan(
+    query_grad, key_terms = over_blocks(
         attention_grads,
         jnp.zeros(queries.shape, jnp.float32),
-        (back_blocks, segment_blocks, block_ids),
+        (key_blocks, segment_blocks, block_ids),
     )
     key_sums = lax.psum_scatter(
         key_terms.reshape(length, seq_count, 2 * key_width).astype(jnp.bfloat16),
@@ -415,22 +482,39 @@
     grad_mixer_in = jnp.dot(normed.T, mixer_grad, preferred_element_type=jnp.float32)
     grad_step_in = jnp.dot(normed.T, step_grad_half, preferred_element_type=jnp.float32)
     normed_grad = (
-        jnp.dot(projected_grad, back_attention_in.T, preferred_element_type=jnp.float32)
-        + jnp.dot(mixer_grad, back_mixer_in.T, preferred_element_type=jnp.float32)
-        + jnp.dot(step_grad_half, back_step_in.T, preferred_element_type=jnp.float32)
+        jnp.dot(projected_grad, full_attention_in.T, preferred_element_type=jnp.float32)
+        + jnp.dot(mixer_grad, full_mixer_in.T, preferred_element_type=jnp.float32)
+        + jnp.dot(step_grad_half, full_step_in.T, preferred_element_type=jnp.float32)
     )
     _, pull_one = jax.vjp(rms_scale, source, gain_mixing)
     source_part, grad_gain_mixing = pull_one(normed_grad)
     input_grad = residual_grad + source_part
-    weight_sums = (
-        lax.psum_scatter(grad_attention_in, ("dp", "ctx"), scatter_dimension=0, tiled=True),
-        lax.psum_scatter(grad_mixer_in, ("dp", "ctx"), scatter_dimension=0, tiled=True),
-        lax.psum_scatter(grad_step_in, ("dp", "ctx"), scatter_dimension=0, tiled=True),
-        lax.psum_scatter(grad_attention_out, ("dp", "ctx"), scatter_dimension=0, tiled=True),
-        lax.psum_scatter(grad_mixer_out, ("dp", "ctx"), scatter_dimension=0, tiled=True),
-        lax.psum_scatter(grad_gate_up, ("dp", "ctx"), scatter_dimension=0, tiled=True),
-        lax.psum_scatter(grad_down_weight, ("dp", "ctx"), scatter_dimension=0, tiled=True),
-    )
+    others = [
+        grad_attention_in.astype(jnp.bfloat16),
+        grad_mixer_in.astype(jnp.bfloat16),
+        fold_rows(grad_attention_out.astype(jnp.bfloat16), attention_out.shape[0], own_rows),
+        fold_rows(grad_mixer_out.astype(jnp.bfloat16), mixer_out.shape[0], own_rows),
+        pad_columns(grad_step_in.astype(jnp.bfloat16)),
+    ]
+    other_sums = lax.psum_scatter(
+        jnp.concatenate(others, axis=1), axes, scatter_dimension=0, tiled=True
+    )
+    feed_parts = cut_columns(
+        feed_sums, (gate_up.shape[1], feed_sums.shape[1] - gate_up.shape[1])
+    )
+    other_parts = cut_columns(other_sums, [part.shape[1] for part in others])
+    weight_sums = [
+        part.astype(jnp.float32)
+        for part in (
+            other_parts[0],
+            other_parts[1],
+            other_parts[4][:, :SSM_HEADS],
+            unfold_rows(other_parts[2], attention_out.shape[0], own_rows, width),
+            unfold_rows(other_parts[3], mixer_out.shape[0], own_rows, width),
+            feed_parts[0],
+            unfold_rows(feed_parts[1], down_weight.shape[0], own_rows, width),
+        )
+    ]
     small_sums = lax.psum(
         (
             grad_gain_mixing,

time: 1610 us -> 662 us (0.41)
  waiting for transfers between devices: 1230 us -> 278 us
  matrix products: 125 us -> 93.8 us
  other arithmetic: 44.3 us -> 65.4 us
  starting transfers between devices: 4.71 us -> 22.7 us
    reduce_scatter x6 -> x2, waiting for transfers between devices: 872 us -> 179 us  [the longest x1 164 us: local(): lax.psum_scatter(jnp.concatenate(others, axis=1), axes, scatter_dimension...]
    all_gather x8 -> x2, waiting for transfers between devices: 321 us -> 52.1 us  [the longest x1 51.5 us: local(): lax.all_gather(entry, axes, axis=0, tiled=True)]
    all_to_all x0 -> x4, waiting for transfers between devices: none -> 46.7 us  [the longest x2 41 us: carried_by_heads(): lax.all_to_all(jnp.concatenate(reached, axis=0), 'ctx', split_axis=0, con...]
    all_gather x2 -> x1, blocking collectives: 51.5 us -> 11.8 us  [local(): decays = lax.all_gather(decay_total, 'ctx')]
    unnamed x18 -> x6, waiting for transfers between devices: 30.9 us -> 0.08 us
    all_gather x1, blocking collectives: 14.8 us -> 38 us  [local(): lax.all_gather(local_keys, 'ctx', axis=0, tiled=True)]
    concatenate x0 -> x10, other arithmetic: none -> 20.9 us  [the longest x1 8.91 us: local(): jnp.concatenate([grad_gate_up, fold_rows(grad_down_weight, down_weight.sh...]
    select_n x14 -> x0, other arithmetic: 18.3 us -> none  [hop(): jnp.where(position < mine, new, old)]
  transfers between devices with their start and end apart: 18 -> 11, of which waited for: 18 -> 8; matrix products, arithmetic and copies ran while one was open for 13% -> 26% of each run, Pallas kernels for 0% -> 0%
where the time goes in v1:
time: 662 us; the launch traced here: 653 us
  waiting for transfers between devices  278 us (42%)
  blocking collectives  107 us (16%)
  matrix products  93.8 us (14%)
  local copies, waits for them, and re-layouts  69.9 us (11%)
  other arithmetic  65.4 us (10%)
  starting transfers between devices  22.7 us (3%)
  between operations  16 us (2%)
    reduce_scatter x1, waiting for transfers between devices, local(): lax.psum_scatter(jnp.concatenate(others, axis=1), axes, scatter_dimension...  164 us
    all_gather x1, waiting for transfers between devices, local(): lax.all_gather(entry, axes, axis=0, tiled=True)  51.5 us
    psum x1, blocking collectives, local(): lax.psum((grad_gain_mixing, grad_gain_feed, pulled[4], pulled[5], pulled[...  43.4 us
    all_to_all x2, waiting for transfers between devices, carried_by_heads(): lax.all_to_all(jnp.concatenate(reached, axis=0), 'ctx', split_axis=0, con...  41 us
    all_gather x1, blocking collectives, local(): lax.all_gather(local_keys, 'ctx', axis=0, tiled=True)  38 us
    unnamed x267, local copies, waits for them, and re-layouts  19.8 us
    reduce_scatter x1, waiting for transfers between devices, local(): lax.psum_scatter(jnp.concatenate([grad_gate_up, fold_rows(grad_down_weigh...  14.9 us
    all_gather x1, blocking collectives, local(): lax.all_gather(local_segments, 'ctx', axis=0, tiled=True)  13.6 us
  transfers between devices with their start and end apart: 11, of which 8 were waited for; matrix products, arithmetic and copies ran while one was open for 26% of the time, Pallas kernels for 0%

profile of v1, /device:TPU:0, one launch (start us, length us, event | category | flops | bytes accessed | tf_op | source)
XLA Modules:
  0.0 652.6 jit_solution(10693826342612042796)
XLA Ops:
  15.4 13.6 %all-gather = s32[1,1024]{1,0:T(1,128)S(1)} all-gather(s32[1,128]{1,0:T(1,128)} %param.18), channel_id=2, replica_groups=mesh['dp'=4,'ctx'=8] {'ctx'}, dimensions={1}, use_global_device_ids=true | all-gather | bytes 4608 | tf_op jit(solution)/shard_map/all_gather | solution.py:251
  41.1 51.5 %all-gather.5.cloned.1.call-done = bf16[1024,4224]{1,0:T(8,128)(2,1)} async-done(((bf16[32,4224]{1,0:T(8,128)(2,1)}), bf16[1024,4224]{1,0:T(8,128)(2,1)}) %all-gather.5.cloned.1.call-update) | async-done | bytes 8650768 | tf_op jit(solution)/shard_map/all_gather | solution.py:222
  94.2 4.1 fusion.7
  105.2 5.5 all-to-all-start
  114.2 38.0 %all-gather.1 = bf16[1024,256]{1,0:T(8,128)(2,1)S(1)} all-gather(bf16[128,256]{1,0:T(8,128)(2,1)S(1)} %slice.457), channel_id=3, replica_groups=mesh['dp'=4,'ctx'=8] {'ctx'}, dimensions={0}, use_global_device_ids=true | all-gather | bytes 589824 | tf_op jit(solution)/shard_map/all_gather | solution.py:250
  154.0 11.8 %all_gather.19 = f32[8,1,24]{2,1,0:T(1,128)S(1)} all-gather(f32[1,1,24]{2,1,0:T(1,128)} %copy.253), channel_id=1, replica_groups=mesh['dp'=4,'ctx'=8] {'ctx'}, dimensions={0}, use_global_device_ids=true | all-gather | bytes 864 | tf_op jit(solution)/shard_map/all_gather | solution.py:333
  166.5 4.2 select_reduce_fusion.1
  178.0 3.6 all-to-all-start.1
  182.4 3.9 select_reduce_fusion
  189.6 34.8 %all-to-all-done.1 = f32[8,3,64,128]{3,2,1,0:T(8,128)S(1)} async-done(((f32[8,3,64,128]{3,2,1,0:T(8,128)}), f32[8,3,64,128]{3,2,1,0:T(8,128)S(1)}, u32[]{:S(2)}, u32[]{:S(2)}) %all-to-all-start.1) | async-done | bytes 786464 | tf_op jit(solution)/shard_map/all_to_all | solution.py:57
  226.1 4.1 fusion.33
  240.8 2.8 fusion.205
  246.3 3.6 pad_maximum_fusion.1
  253.7 3.5 multiply_reduce_fusion.9
  265.4 3.6 convolution_convert_fusion.6
  269.1 5.7 convolution_convert_fusion.1
  286.6 8.9 %pad_maximum_fusion = bf16[1024,6144]{1,0:T(8,128)(2,1)} fusion(bf16[1024,2048]{1,0:T(8,128)(2,1)S(1)} %bitcast.449, bf16[1024,4096]{1,0:T(8,128)(2,1)S(1)} %bitcast.430), kind=kLoop, calls=%fused_computation.6 | loop fusion | flops 25165824 | bytes 25165824 | tf_op jit(solution)/shard_map/concatenate | solution.py:366
  297.4 5.5 fusion.71
  311.6 4.5 all-to-all-start.2
  318.6 4.3 fusion.50
  331.2 5.7 all-to-all-done.2
  342.3 4.2 all-to-all-start.3
  358.6 2.8 constant_dynamic-update-slice_fusion.12
  361.4 6.1 all-to-all-done.3
  370.1 3.5 fusion.27
  381.0 3.6 fusion.198
  388.9 4.9 fusion
  398.8 3.6 fusion.44
  402.6 5.3 fusion.5
  411.6 43.4 %all-reduce.4 = (f32[1024]{0:T(1024)}, f32[1024]{0:T(1024)}, f32[24]{0:T(128)}, f32[24]{0:T(128)}, f32[24]{0:T(128)}, /*index=5*/f32[4,1792]{1,0:T(4,128)}, f32[1792]{0:T(1024)}) all-reduce(f32[1024]{0:T(1024)S(1)} %get-tuple-element.126, f32[1024]{0:T(1024)S(1)} %copy-done.106, ...), channel_id=1, replica_groups=mesh['dp'=4,'ctx'=8] {'dp','ctx'}, use_global_device_ids=true, to_apply=%region_21.22 | all-reduce | flops 11080 | bytes 88640 | tf_op jit(solution)/shard_map/psum | solution.py:518
  456.1 14.9 %reduce-scatter.8.cloned.1.call-done = bf16[32,6144]{1,0:T(8,128)(2,1)} async-done(((bf16[1024,6144]{1,0:T(8,128)(2,1)}), bf16[32,6144]{1,0:T(8,128)(2,1)}) %reduce-scatter.8.cloned.1.call-update) | async-done | bytes 393232 | tf_op jit(solution)/shard_map/reduce_scatter | solution.py:365
  474.4 164.0 %reduce-scatter.6.cloned.1.call-done = bf16[32,6272]{1,0:T(8,128)(2,1)} async-done(((bf16[1024,6272]{1,0:T(8,128)(2,1)}), bf16[32,6272]{1,0:T(8,128)(2,1)}) %reduce-scatter.6.cloned.1.call-update) | async-done | bytes 401424 | tf_op jit(solution)/shard_map/reduce_scatter | solution.py:499
  (463 shorter events, 157.2 us)
Async XLA Ops:
  7.2 85.3 %copy-start.49 = (f32[1024]{0:T(1024)S(1)}, f32[1024]{0:T(1024)}, u32[]{:S(2)}) copy-start(f32[1024]{0:T(1024)} %param.27) | copy-start | bytes 12292
  7.2 85.3 %copy-start.119 = (f32[24]{0:T(128)S(1)}, f32[24]{0:T(128)}, u32[]{:S(2)}) copy-start(f32[24]{0:T(128)} %param.30) | copy-start | bytes 292
  7.2 85.3 %all-gather.5.cloned.1.call-start = ((), (), s32[]{:S(2)}) async-start(), calls=%async_computation.7 | async-start | bytes 8921088 | tf_op jit(solution)/shard_map/all_gather | solution.py:222
  9.8 225.2 %all-gather.7.cloned.1.call-start = ((), (), s32[]{:S(2)}) async-start(), calls=%async_computation.8 | async-start | bytes 17301504 | tf_op jit(solution)/shard_map/all_gather | solution.py:227
  36.6 64.0 %copy-start.84 = (pred[128]{0:T(512)(128)(4,1)}, pred[128]{0:T(512)(128)(4,1)S(1)}, u32[]{:S(2)}) copy-start(pred[128]{0:T(512)(128)(4,1)S(1)} %get-tuple-element.218) | copy-start | bytes 388
  36.6 64.8 %copy-start.103 = (pred[128]{0:T(512)(128)(4,1)}, pred[128]{0:T(512)(128)(4,1)S(1)}, u32[]{:S(2)}) copy-start(pred[128]{0:T(512)(128)(4,1)S(1)} %get-tuple-element.219) | copy-start | bytes 388
  36.6 64.8 %copy-start.104 = (pred[128]{0:T(512)(128)(4,1)}, pred[128]{0:T(512)(128)(4,1)S(1)}, u32[]{:S(2)}) copy-start(pred[128]{0:T(512)(128)(4,1)S(1)} %get-tuple-element.220) | copy-start | bytes 388
  36.6 64.8 %copy-start.105 = (pred[1,128]{1,0:T(4,128)(4,1)}, pred[1,128]{1,0:T(4,128)(4,1)S(1)}, u32[]{:S(2)}) copy-start(pred[1,128]{1,0:T(4,128)(4,1)S(1)} %get-tuple-element.222) | copy-start | bytes 388
  37.0 63.6 %copy-start.95 = (pred[128]{0:T(512)(128)(4,1)}, pred[128]{0:T(512)(128)(4,1)S(1)}, u32[]{:S(2)}) copy-start(pred[128]{0:T(512)(128)(4,1)S(1)} %compare_reduce_fusion) | copy-start | bytes 388
  38.3 63.1 %copy-start.63 = (f32[1792]{0:T(1024)}, f32[1792]{0:T(1024)S(1)}, u32[]{:S(2)}) copy-start(f32[1792]{0:T(1024)S(1)} %get-tuple-element.128) | copy-start | bytes 21508
  38.3 63.1 %copy-start.65 = (f32[1792]{0:T(1024)}, f32[1792]{0:T(1024)S(1)}, u32[]{:S(2)}) copy-start(f32[1792]{0:T(1024)S(1)} %get-tuple-element.129) | copy-start | bytes 21508
  38.3 63.1 %copy-start.67 = (f32[1792]{0:T(1024)}, f32[1792]{0:T(1024)S(1)}, u32[]{:S(2)}) copy-start(f32[1792]{0:T(1024)S(1)} %get-tuple-element.130) | copy-start | bytes 21508
  38.3 63.1 %copy-start.69 = (f32[1792]{0:T(1024)}, f32[1792]{0:T(1024)S(1)}, u32[]{:S(2)}) copy-start(f32[1792]{0:T(1024)S(1)} %get-tuple-element.131) | copy-start | bytes 21508
  38.5 55.4 %copy-start.114 = (f32[24]{0:T(128)}, f32[24]{0:T(128)S(1)}, u32[]{:S(2)}) copy-start(f32[24]{0:T(128)S(1)} %exponential_negate_fusion) | copy-start | bytes 292
  39.1 71.6 %copy-start.73 = (f32[128]{0:T(128)}, f32[128]{0:T(128)S(1)}, u32[]{:S(2)}) copy-start(f32[128]{0:T(128)S(1)} %fusion.179) | copy-start | bytes 1540
  98.4 3.0 collective-permute-start
  103.2 86.1 %copy-start.10 = (f32[1,128,1792]{2,1,0:T(8,128)}, f32[1,128,1792]{2,1,0:T(8,128)S(1)}, u32[]{:S(2)}) copy-start(f32[1,128,1792]{2,1,0:T(8,128)S(1)} %get-tuple-element.158) | copy-start | bytes 2752516
  105.2 65.4 %all-to-all-start = ((f32[1,24,64,128]{3,2,0,1:T(8,128)}), f32[1,24,64,128]{3,2,0,1:T(8,128)S(1)}, u32[]{:S(2)}, u32[]{:S(2)}) async-start(f32[1,24,64,128]{3,2,0,1:T(8,128)} %convolution_bitcast_fusion.3), calls=%async_computation | async-start | bytes 1572864 | tf_op jit(solution)/shard_map/all_to_all | solution.py:49
  114.2 57.2 %copy-start.33 = (bf16[2,512,64]{1,2,0:T(8,128)(2,1)}, bf16[2,512,64]{1,2,0:T(8,128)(2,1)S(1)}, u32[]{:S(2)}) copy-start(bf16[2,512,64]{1,2,0:T(8,128)(2,1)S(1)} %reshape.1164) | copy-start | bytes 393220
  178.0 46.5 %all-to-all-start.1 = ((f32[8,3,64,128]{3,2,1,0:T(8,128)}), f32[8,3,64,128]{3,2,1,0:T(8,128)S(1)}, u32[]{:S(2)}, u32[]{:S(2)}) async-start(f32[8,3,64,128]{3,2,1,0:T(8,128)} %copy.255), calls=%async_computation.1 | async-start | bytes 1572864 | tf_op jit(solution)/shard_map/all_to_all | solution.py:57
  181.5 171.6 %reduce-scatter.10.cloned.1.call-start = ((), (), s32[]{:S(2)}) async-start(), calls=%async_computation.11 | async-start | bytes 589824
  189.3 54.4 %copy-start.23 = (bf16[1,2,4,128,64]{3,4,2,1,0:T(8,128)(2,1)}, bf16[1,2,4,128,64]{3,4,2,1,0:T(8,128)(2,1)S(1)}, u32[]{:S(2)}) copy-start(bf16[1,2,4,128,64]{3,4,2,1,0:T(8,128)(2,1)S(1)} %copy.244) | copy-start | bytes 393220
  281.5 189.5 %reduce-scatter.8.cloned.1.call-start = ((), (), s32[]{:S(2)}) async-start(), calls=%async_computation.10 | async-start | bytes 12976128 | tf_op jit(solution)/shard_map/reduce_scatter | solution.py:365
  311.6 25.4 %all-to-all-start.2 = ((f32[1,24,64,128]{3,2,0,1:T(8,128)}), f32[1,24,64,128]{3,2,0,1:T(8,128)}, u32[]{:S(2)}, u32[]{:S(2)}) async-start(f32[1,24,64,128]{3,2,0,1:T(8,128)} %convolution_bitcast_fusion.2), calls=%async_computation.2 | async-start | bytes 1572864 | tf_op jit(solution)/shard_map/all_to_all | solution.py:49
  342.3 25.2 %all-to-all-start.3 = ((f32[8,3,64,128]{3,2,1,0:T(8,128)}), f32[8,3,64,128]{3,2,1,0:T(8,128)}, u32[]{:S(2)}, u32[]{:S(2)}) async-start(f32[8,3,64,128]{3,2,1,0:T(8,128)} %copy.264), calls=%async_computation.3 | async-start | bytes 1572864 | tf_op jit(solution)/shard_map/all_to_all | solution.py:57
  346.6 291.8 %reduce-scatter.6.cloned.1.call-start = ((), (), s32[]{:S(2)}) async-start(), calls=%async_computation.9 | async-start | bytes 13246464 | tf_op jit(solution)/shard_map/reduce_scatter | solution.py:499
  384.6 3.6 collective-permute-start.1
  408.0 46.9 %copy-start.118 = (f32[128]{0:T(128)S(1)}, f32[128]{0:T(128)}, u32[]{:S(2)}) copy-start(f32[128]{0:T(128)} %copy-done.117) | copy-start | bytes 1540
  408.0 46.9 %copy-start.19 = (bf16[1,128,1024]{2,1,0:T(8,128)(2,1)S(1)}, bf16[1,128,1024]{2,1,0:T(8,128)(2,1)}, u32[]{:S(2)}) copy-start(bf16[1,128,1024]{2,1,0:T(8,128)(2,1)} %param.19) | copy-start | bytes 786436
  408.0 46.9 %copy-start.22 = (f32[128,1024]{1,0:T(8,128)S(1)}, f32[128,1024]{1,0:T(8,128)}, u32[]{:S(2)}) copy-start(f32[128,1024]{1,0:T(8,128)} %copy-done.21) | copy-start | bytes 1572868
  408.0 46.9 %copy-start.56 = (f32[1024]{0:T(1024)S(1)}, f32[1024]{0:T(1024)}, u32[]{:S(2)}) copy-start(f32[1024]{0:T(1024)} %param.28) | copy-start | bytes 12292
  408.1 46.9 %copy-start.83 = (f32[128]{0:T(128)S(1)}, f32[128]{0:T(128)}, u32[]{:S(2)}) copy-start(f32[128]{0:T(128)} %copy-done.81) | copy-start | bytes 1540
  (109 other events, 1200.9 us)
Sparse Core Ops, SparseCore 0:
  11.6 80.8 all-gather.4
  96.1 138.8 all-gather.6
  281.6 30.2 reduce-scatter.9
  317.7 153.1 reduce-scatter.7
  473.1 165.2 reduce-scatter.5

commit v2 on v1

--- a/solution.py
+++ b/solution.py
@@ -362,19 +362,15 @@
     grad_gate_up = jnp.dot(normed_two.T, gate_grad, preferred_element_type=jnp.float32).astype(
         jnp.bfloat16
     )
-    feed_sums = lax.psum_scatter(
-        jnp.concatenate(
-            [grad_gate_up, fold_rows(grad_down_weight, down_weight.shape[0], own_rows)], axis=1
-        ),
-        axes,
-        scatter_dimension=0,
-        tiled=True,
-    )
+    feed_terms = jnp.concatenate(
+        [grad_gate_up, fold_rows(grad_down_weight, down_weight.shape[0], own_rows)], axis=1
+    )
+    feed_sums = lax.psum_scatter(feed_terms, axes, scatter_dimension=0, tiled=True)
     normed_two_grad = jnp.dot(gate_grad, full_gate_up.T, preferred_element_type=jnp.float32)
     _, pull_two = jax.vjp(rms_scale, residual, gain_feed)
     residual_part, grad_gain_feed = pull_two(normed_two_grad)
     residual_grad = cotangent.astype(jnp.float32) + residual_part
-    residual_half = residual_grad.astype(jnp.bfloat16)
+    residual_half, _ = lax.optimization_barrier((residual_grad.astype(jnp.bfloat16), feed_terms))
     grad_attention_out = jnp.dot(attended_flat.T, residual_half, preferred_element_type=jnp.float32)
     grad_mixer_out = jnp.dot(gated.T, residual_half, preferred_element_type=jnp.float32)
     attended_grad = jnp.dot(
@@ -468,12 +464,16 @@
         jnp.zeros(queries.shape, jnp.float32),
         (key_blocks, segment_blocks, block_ids),
     )
-    key_sums = lax.psum_scatter(
+    key_pieces = lax.all_to_all(
         key_terms.reshape(length, seq_count, 2 * key_width).astype(jnp.bfloat16),
         "ctx",
-        scatter_dimension=0,
+        split_axis=0,
+        concat_axis=0,
         tiled=True,
-    ).astype(jnp.float32)
+    )
+    key_sums = jnp.sum(
+        key_pieces.reshape(-1, tok_count, seq_count, 2 * key_width).astype(jnp.float32), axis=0
+    )
     kv_grad = key_sums.transpose(1, 0, 2).reshape(row_count, 2 * key_width)
     projected_grad = jnp.concatenate(
         [ungroup(query_grad, seq_count, tok_count), kv_grad], axis=1

time: 662 us -> 654 us (0.988)
  waiting for transfers between devices: 278 us -> 244 us
  other arithmetic: 65.4 us -> 75.2 us
    reduce_scatter x1, waiting for transfers between devices: 164 us -> 103 us  [local(): lax.psum_scatter(jnp.concatenate(others, axis=1), axes, scatter_dimension...]
    all_to_all x2, waiting for transfers between devices: 5.75 us -> 26.6 us  [carried_by_heads(): lax.all_to_all(state, 'ctx', split_axis=1, concat_axis=0, tiled=True)]
    reduce_scatter x1, waiting for transfers between devices: 14.9 us -> 0.01 us  [local(): lax.psum_scatter(feed_terms, axes, scatter_dimension=0, tiled=True)]
    all_to_all x2, waiting for transfers between devices: 41 us -> 52.4 us  [carried_by_heads(): lax.all_to_all(jnp.concatenate(reached, axis=0), 'ctx', split_axis=0, con...]
    all_to_all x0 -> x1, waiting for transfers between devices: none -> 9.91 us  [local(): lax.all_to_all(key_terms.reshape(length, seq_count, 2 * key_width).astype...]
    concatenate x0 -> x2, other arithmetic: none -> 9.68 us  [attention_grads(): jnp.concatenate([key_grad.reshape(block, seq_count, key_width), value_gra...]
    unnamed x267 -> x263, local copies, waits for them, and re-layouts: 19.8 us -> 22 us
  transfers between devices with their start and end apart: 11 -> 11, of which waited for: 8 -> 8; matrix products, arithmetic and copies ran while one was open for 26% -> 32% of each run, Pallas kernels for 0% -> 0%
where the time goes in v2:
time: 654 us; the launch traced here: 644 us
  waiting for transfers between devices  244 us (37%)
  blocking collectives  108 us (17%)
  matrix products  99.1 us (15%)
  local copies, waits for them, and re-layouts  75.3 us (12%)
  other arithmetic  75.2 us (11%)
  starting transfers between devices  25.9 us (4%)
  between operations  16.3 us (2%)
    reduce_scatter x1, waiting for transfers between devices, local(): lax.psum_scatter(jnp.concatenate(others, axis=1), axes, scatter_dimension...  103 us
    all_to_all x2, waiting for transfers between devices, carried_by_heads(): lax.all_to_all(jnp.concatenate(reached, axis=0), 'ctx', split_axis=0, con...  52.4 us
    all_gather x1, waiting for transfers between devices, local(): lax.all_gather(entry, axes, axis=0, tiled=True)  51.6 us
    psum x1, blocking collectives, local(): lax.psum((grad_gain_mixing, grad_gain_feed, pulled[4], pulled[5], pulled[...  44.3 us
    all_gather x1, blocking collectives, local(): lax.all_gather(local_keys, 'ctx', axis=0, tiled=True)  38 us
    all_to_all x2, waiting for transfers between devices, carried_by_heads(): lax.all_to_all(state, 'ctx', split_axis=1, concat_axis=0, tiled=True)  26.6 us
    unnamed x263, local copies, waits for them, and re-layouts  22 us
    all_gather x1, blocking collectives, local(): lax.all_gather(local_segments, 'ctx', axis=0, tiled=True)  13.6 us
  transfers between devices with their start and end apart: 11, of which 8 were waited for; matrix products, arithmetic and copies ran while one was open for 32% of the time, Pallas kernels for 0%

profile of v2, /device:TPU:0, one launch (start us, length us, event | category | flops | bytes accessed | tf_op | source)
XLA Modules:
  0.0 643.8 jit_solution(12425481286139073236)
XLA Ops:
  15.4 13.6 %all-gather = s32[1,1024]{1,0:T(1,128)S(1)} all-gather(s32[1,128]{1,0:T(1,128)} %param.18), channel_id=2, replica_groups=mesh['dp'=4,'ctx'=8] {'ctx'}, dimensions={1}, use_global_device_ids=true | all-gather | bytes 4608 | tf_op jit(solution)/shard_map/all_gather | solution.py:251
  41.0 51.6 %all-gather.5.cloned.1.call-done = bf16[1024,4224]{1,0:T(8,128)(2,1)} async-done(((bf16[32,4224]{1,0:T(8,128)(2,1)}), bf16[1024,4224]{1,0:T(8,128)(2,1)}) %all-gather.5.cloned.1.call-update) | async-done | bytes 8650768 | tf_op jit(solution)/shard_map/all_gather | solution.py:222
  94.2 4.1 fusion.7
  105.3 5.5 all-to-all-start
  114.3 38.0 %all-gather.1 = bf16[1024,256]{1,0:T(8,128)(2,1)S(1)} all-gather(bf16[128,256]{1,0:T(8,128)(2,1)S(1)} %slice.457), channel_id=3, replica_groups=mesh['dp'=4,'ctx'=8] {'ctx'}, dimensions={0}, use_global_device_ids=true | all-gather | bytes 589824 | tf_op jit(solution)/shard_map/all_gather | solution.py:250
  154.1 11.8 %all_gather.19 = f32[8,1,24]{2,1,0:T(1,128)S(1)} all-gather(f32[1,1,24]{2,1,0:T(1,128)} %copy.304), channel_id=1, replica_groups=mesh['dp'=4,'ctx'=8] {'ctx'}, dimensions={0}, use_global_device_ids=true | all-gather | bytes 864 | tf_op jit(solution)/shard_map/all_gather | solution.py:333
  166.5 4.3 select_reduce_fusion.1
  178.0 3.6 all-to-all-start.1
  182.0 3.9 select_reduce_fusion
  189.3 35.1 %all-to-all-done.1 = f32[8,3,64,128]{3,2,1,0:T(8,128)S(1)} async-done(((f32[8,3,64,128]{3,2,1,0:T(8,128)}), f32[8,3,64,128]{3,2,1,0:T(8,128)S(1)}, u32[]{:S(2)}, u32[]{:S(2)}) %all-to-all-start.1) | async-done | bytes 786464 | tf_op jit(solution)/shard_map/all_to_all | solution.py:57
  226.1 4.1 fusion.33
  257.5 9.2 %pad_maximum_fusion = bf16[1024,6144]{1,0:T(8,128)(2,1)} fusion(bf16[1024,2048]{1,0:T(8,128)(2,1)S(1)} %bitcast.442, bf16[1024,4096]{1,0:T(8,128)(2,1)S(1)} %convolution_convert_fusion.1), kind=kLoop, calls=%fused_computation.6 | loop fusion | flops 25165824 | bytes 25165824 | tf_op jit(solution)/shard_map/concatenate | solution.py:365
  268.6 7.7 %multiply_reduce_fusion.9 = (f32[1024]{0:T(1024)}, f32[128]{0:T(128)S(1)}, f32[128,1024]{1,0:T(8,128)S(1)}) fusion(f32[128,1024]{1,0:T(8,128)S(1)} %get-tuple-element.246, f32[128]{0:T(128)S(1)} %fusion.180, f32[1024]{0:T(1024)S(1)} %copy-done.54, bf16[1024,8192]{1,0:T(8,128)(2,1)} %all-gather.7.cloned.1.call-done, bf16[128,2048]{1,0:T(8,128)(2,1)} %copy-done.33, ...), kind=kOutput, calls=%fused_computation.173 | convolution fusion | flops 1076624256 | bytes 10494976 | tf_op jit(solution)/shard_map/dot_general | solution.py:369
  276.6 4.1 fusion.71
  294.4 4.6 convolution_convert_fusion.6
  301.9 4.3 multiply_convert_fusion
  310.9 4.1 pad_maximum_fusion.5
  315.5 5.6 reduce.52
  325.7 4.4 all-to-all-start.3
  332.7 4.3 fusion.50
  345.3 26.6 %all-to-all-done.3 = f32[1,24,64,128]{3,2,0,1:T(8,128)} async-done(((f32[1,24,64,128]{3,2,0,1:T(8,128)}), f32[1,24,64,128]{3,2,0,1:T(8,128)}, u32[]{:S(2)}, u32[]{:S(2)}) %all-to-all-start.3) | async-done | bytes 786464 | tf_op jit(solution)/shard_map/all_to_all | solution.py:49
  371.9 4.1 all-to-all-start.2
  381.5 9.9 %all-to-all-done.2 = bf16[8,2,16384]{2,1,0:T(2,128)(2,1)} async-done(((bf16[8,2,16384]{2,1,0:T(2,128)(2,1)}), bf16[8,2,16384]{2,1,0:T(2,128)(2,1)}, u32[]{:S(2)}, u32[]{:S(2)}) %all-to-all-start.2) | async-done | bytes 524320 | tf_op jit(solution)/shard_map/all_to_all | solution.py:467
  391.4 4.2 all-to-all-start.4
  415.7 17.3 %all-to-all-done.4 = f32[8,3,64,128]{3,2,1,0:T(8,128)} async-done(((f32[8,3,64,128]{3,2,1,0:T(8,128)}), f32[8,3,64,128]{3,2,1,0:T(8,128)}, u32[]{:S(2)}, u32[]{:S(2)}) %all-to-all-start.4) | async-done | bytes 786464 | tf_op jit(solution)/shard_map/all_to_all | solution.py:57
  435.5 3.5 fusion.27
  446.5 3.6 fusion.198
  454.6 4.9 fusion
  464.3 3.6 fusion.44
  468.2 5.5 fusion.5
  477.2 44.3 %all-reduce.4 = (f32[1024]{0:T(1024)}, f32[1024]{0:T(1024)}, f32[24]{0:T(128)}, f32[24]{0:T(128)}, f32[24]{0:T(128)}, /*index=5*/f32[4,1792]{1,0:T(4,128)}, f32[1792]{0:T(1024)}) all-reduce(f32[1024]{0:T(1024)S(1)} %get-tuple-element.144, f32[1024]{0:T(1024)S(1)} %copy-done.104, ...), channel_id=1, replica_groups=mesh['dp'=4,'ctx'=8] {'dp','ctx'}, use_global_device_ids=true, to_apply=%region_21.22 | all-reduce | flops 11080 | bytes 88640 | tf_op jit(solution)/shard_map/psum | solution.py:518
  526.2 103.1 %reduce-scatter.3.cloned.1.call-done = bf16[32,6272]{1,0:T(8,128)(2,1)} async-done(((bf16[1024,6272]{1,0:T(8,128)(2,1)}), bf16[32,6272]{1,0:T(8,128)(2,1)}) %reduce-scatter.3.cloned.1.call-update) | async-done | bytes 401424 | tf_op jit(solution)/shard_map/reduce_scatter | solution.py:499
  (462 shorter events, 173.2 us)
Async XLA Ops:
  7.2 85.4 %copy-start.48 = (f32[1024]{0:T(1024)S(1)}, f32[1024]{0:T(1024)}, u32[]{:S(2)}) copy-start(f32[1024]{0:T(1024)} %param.27) | copy-start | bytes 12292
  7.2 85.4 %copy-start.118 = (f32[24]{0:T(128)S(1)}, f32[24]{0:T(128)}, u32[]{:S(2)}) copy-start(f32[24]{0:T(128)} %param.30) | copy-start | bytes 292
  7.2 85.3 %all-gather.5.cloned.1.call-start = ((), (), s32[]{:S(2)}) async-start(), calls=%async_computation.7 | async-start | bytes 8921088 | tf_op jit(solution)/shard_map/all_gather | solution.py:222
  9.8 225.2 %all-gather.7.cloned.1.call-start = ((), (), s32[]{:S(2)}) async-start(), calls=%async_computation.8 | async-start | bytes 17301504 | tf_op jit(solution)/shard_map/all_gather | solution.py:227
  36.6 64.0 %copy-start.82 = (pred[128]{0:T(512)(128)(4,1)}, pred[128]{0:T(512)(128)(4,1)S(1)}, u32[]{:S(2)}) copy-start(pred[128]{0:T(512)(128)(4,1)S(1)} %get-tuple-element.236) | copy-start | bytes 388
  36.6 64.8 %copy-start.101 = (pred[128]{0:T(512)(128)(4,1)}, pred[128]{0:T(512)(128)(4,1)S(1)}, u32[]{:S(2)}) copy-start(pred[128]{0:T(512)(128)(4,1)S(1)} %get-tuple-element.237) | copy-start | bytes 388
  36.6 64.9 %copy-start.102 = (pred[128]{0:T(512)(128)(4,1)}, pred[128]{0:T(512)(128)(4,1)S(1)}, u32[]{:S(2)}) copy-start(pred[128]{0:T(512)(128)(4,1)S(1)} %get-tuple-element.238) | copy-start | bytes 388
  36.6 64.9 %copy-start.103 = (pred[1,128]{1,0:T(4,128)(4,1)}, pred[1,128]{1,0:T(4,128)(4,1)S(1)}, u32[]{:S(2)}) copy-start(pred[1,128]{1,0:T(4,128)(4,1)S(1)} %get-tuple-element.240) | copy-start | bytes 388
  37.0 63.6 %copy-start.93 = (pred[128]{0:T(512)(128)(4,1)}, pred[128]{0:T(512)(128)(4,1)S(1)}, u32[]{:S(2)}) copy-start(pred[128]{0:T(512)(128)(4,1)S(1)} %compare_reduce_fusion) | copy-start | bytes 388
  38.3 63.1 %copy-start.62 = (f32[1792]{0:T(1024)}, f32[1792]{0:T(1024)S(1)}, u32[]{:S(2)}) copy-start(f32[1792]{0:T(1024)S(1)} %get-tuple-element.146) | copy-start | bytes 21508
  38.3 63.1 %copy-start.64 = (f32[1792]{0:T(1024)}, f32[1792]{0:T(1024)S(1)}, u32[]{:S(2)}) copy-start(f32[1792]{0:T(1024)S(1)} %get-tuple-element.147) | copy-start | bytes 21508
  38.3 63.1 %copy-start.66 = (f32[1792]{0:T(1024)}, f32[1792]{0:T(1024)S(1)}, u32[]{:S(2)}) copy-start(f32[1792]{0:T(1024)S(1)} %get-tuple-element.148) | copy-start | bytes 21508
  38.3 63.1 %copy-start.68 = (f32[1792]{0:T(1024)}, f32[1792]{0:T(1024)S(1)}, u32[]{:S(2)}) copy-start(f32[1792]{0:T(1024)S(1)} %get-tuple-element.149) | copy-start | bytes 21508
  38.5 55.5 %copy-start.111 = (f32[24]{0:T(128)}, f32[24]{0:T(128)S(1)}, u32[]{:S(2)}) copy-start(f32[24]{0:T(128)S(1)} %exponential_negate_fusion) | copy-start | bytes 292
  39.0 71.8 %copy-start.72 = (f32[128]{0:T(128)}, f32[128]{0:T(128)S(1)}, u32[]{:S(2)}) copy-start(f32[128]{0:T(128)S(1)} %fusion.179) | copy-start | bytes 1540
  98.4 3.0 collective-permute-start
  103.3 85.8 %copy-start.12 = (f32[1,128,1792]{2,1,0:T(8,128)}, f32[1,128,1792]{2,1,0:T(8,128)S(1)}, u32[]{:S(2)}) copy-start(f32[1,128,1792]{2,1,0:T(8,128)S(1)} %get-tuple-element.176) | copy-start | bytes 2752516
  105.3 65.5 %all-to-all-start = ((f32[1,24,64,128]{3,2,0,1:T(8,128)}), f32[1,24,64,128]{3,2,0,1:T(8,128)S(1)}, u32[]{:S(2)}, u32[]{:S(2)}) async-start(f32[1,24,64,128]{3,2,0,1:T(8,128)} %convolution_bitcast_fusion.3), calls=%async_computation | async-start | bytes 1572864 | tf_op jit(solution)/shard_map/all_to_all | solution.py:49
  114.3 57.2 %copy-start.34 = (bf16[2,512,64]{1,2,0:T(8,128)(2,1)}, bf16[2,512,64]{1,2,0:T(8,128)(2,1)S(1)}, u32[]{:S(2)}) copy-start(bf16[2,512,64]{1,2,0:T(8,128)(2,1)S(1)} %reshape.1182) | copy-start | bytes 393220
  178.0 46.5 %all-to-all-start.1 = ((f32[8,3,64,128]{3,2,1,0:T(8,128)}), f32[8,3,64,128]{3,2,1,0:T(8,128)S(1)}, u32[]{:S(2)}, u32[]{:S(2)}) async-start(f32[8,3,64,128]{3,2,1,0:T(8,128)} %copy.306), calls=%async_computation.1 | async-start | bytes 1572864 | tf_op jit(solution)/shard_map/all_to_all | solution.py:57
  181.5 341.2 %reduce-scatter.5.cloned.1.call-start = ((), (), s32[]{:S(2)}) async-start(), calls=%async_computation.10 | async-start | bytes 12976128 | tf_op jit(solution)/shard_map/reduce_scatter | solution.py:368
  189.0 53.9 %copy-start.26 = (bf16[1,2,4,128,64]{3,4,2,1,0:T(8,128)(2,1)}, bf16[1,2,4,128,64]{3,4,2,1,0:T(8,128)(2,1)S(1)}, u32[]{:S(2)}) copy-start(bf16[1,2,4,128,64]{3,4,2,1,0:T(8,128)(2,1)S(1)} %copy.295) | copy-start | bytes 393220
  325.7 46.2 %all-to-all-start.3 = ((f32[1,24,64,128]{3,2,0,1:T(8,128)}), f32[1,24,64,128]{3,2,0,1:T(8,128)}, u32[]{:S(2)}, u32[]{:S(2)}) async-start(f32[1,24,64,128]{3,2,0,1:T(8,128)} %convolution_bitcast_fusion.2), calls=%async_computation.3 | async-start | bytes 1572864 | tf_op jit(solution)/shard_map/all_to_all | solution.py:49
  345.3 52.2 %copy-start.36 = (bf16[2,512,64]{1,2,0:T(8,128)(2,1)S(1)}, bf16[2,512,64]{1,2,0:T(8,128)(2,1)}, u32[]{:S(2)}) copy-start(bf16[2,512,64]{1,2,0:T(8,128)(2,1)} %fusion.45) | copy-start | bytes 393220
  371.9 19.5 %all-to-all-start.2 = ((bf16[8,2,16384]{2,1,0:T(2,128)(2,1)}), bf16[8,2,16384]{2,1,0:T(2,128)(2,1)}, u32[]{:S(2)}, u32[]{:S(2)}) async-start(bf16[8,2,16384]{2,1,0:T(2,128)(2,1)} %reshape.1330), calls=%async_computation.2 | async-start | bytes 1048576 | tf_op jit(solution)/shard_map/all_to_all | solution.py:467
  391.4 41.6 %all-to-all-start.4 = ((f32[8,3,64,128]{3,2,1,0:T(8,128)}), f32[8,3,64,128]{3,2,1,0:T(8,128)}, u32[]{:S(2)}, u32[]{:S(2)}) async-start(f32[8,3,64,128]{3,2,1,0:T(8,128)} %copy.318), calls=%async_computation.4 | async-start | bytes 1572864 | tf_op jit(solution)/shard_map/all_to_all | solution.py:57
  395.6 233.7 %reduce-scatter.3.cloned.1.call-start = ((), (), s32[]{:S(2)}) async-start(), calls=%async_computation.9 | async-start | bytes 13246464 | tf_op jit(solution)/shard_map/reduce_scatter | solution.py:499
  450.1 3.7 collective-permute-start.1
  473.7 47.9 %copy-start.115 = (f32[128]{0:T(128)S(1)}, f32[128]{0:T(128)}, u32[]{:S(2)}) copy-start(f32[128]{0:T(128)} %copy-done.114) | copy-start | bytes 1540
  473.7 47.9 %copy-start.23 = (bf16[1,128,1024]{2,1,0:T(8,128)(2,1)S(1)}, bf16[1,128,1024]{2,1,0:T(8,128)(2,1)}, u32[]{:S(2)}) copy-start(bf16[1,128,1024]{2,1,0:T(8,128)(2,1)} %param.19) | copy-start | bytes 786436
  473.7 47.9 %copy-start.25 = (f32[128,1024]{1,0:T(8,128)S(1)}, f32[128,1024]{1,0:T(8,128)}, u32[]{:S(2)}) copy-start(f32[128,1024]{1,0:T(8,128)} %copy-done.24) | copy-start | bytes 1572868
  473.7 47.9 %copy-start.55 = (f32[1024]{0:T(1024)S(1)}, f32[1024]{0:T(1024)}, u32[]{:S(2)}) copy-start(f32[1024]{0:T(1024)} %param.28) | copy-start | bytes 12292
  (106 other events, 1421.2 us)
Sparse Core Ops, SparseCore 0:
  11.6 80.9 all-gather.4
  96.2 138.7 all-gather.6
  266.8 187.2 reduce-scatter.4
  463.4 165.8 reduce-scatter.2
